TPU v7x, 32 devices: a whole 2x2x4 slice. The times are simulated.
32 devices in a mesh: dp: 4 (over y, x), ctx: 2 (over core), tensor: 4 (over z).
Axes of the slice: x: 2, y: 2, z: 4, core: 2. Of those that a mesh axis runs over, the one named last changes fastest.
Arguments:
- inputs: bfloat16 [4, 1024, 2048], P('dp', 'ctx'), may hold values from -6 to 6
- segment_ids: int32 [4, 1024], P('dp', 'ctx'), may hold values from -1 to 1022, as said below
- attention_gain: float32 [2048], replicated, may hold values from 0.5 to 1.5
- query_weight: bfloat16 [2048, 2048], P(None, 'tensor'), may hold values from -0.125 to 0.125
- key_weight: bfloat16 [2048, 256], P(None, 'tensor'), may hold values from -0.125 to 0.125
- value_weight: bfloat16 [2048, 256], P(None, 'tensor'), may hold values from -0.125 to 0.125
- out_weight: bfloat16 [2048, 2048], P('tensor'), may hold values from -0.75 to 0.75
- feedforward_gain: float32 [2048], replicated, may hold values from 0.5 to 1.5
- gate_weight: bfloat16 [2048, 5632], P(None, 'tensor'), may hold values from -0.125 to 0.125
- up_weight: bfloat16 [2048, 5632], P(None, 'tensor'), may hold values from -0.125 to 0.125
- down_weight: bfloat16 [5632, 2048], P('tensor'), may hold values from -0.078125 to 0.078125
- cotangent: bfloat16 [4, 1024, 2048], P('dp', 'ctx'), may hold values from -6 to 6
Outputs:
- layer_out: bfloat16 [4, 1024, 2048], P('dp', 'ctx')
- grad_inputs: bfloat16 [4, 1024, 2048], P('dp', 'ctx')
- grad_attention_gain: float32 [2048], P(('dp', 'ctx'))
- grad_query_weight: float32 [2048, 2048], P(('dp', 'ctx'), 'tensor')
- grad_key_weight: float32 [2048, 256], P(('dp', 'ctx'), 'tensor')
- grad_value_weight: float32 [2048, 256], P(('dp', 'ctx'), 'tensor')
- grad_out_weight: float32 [2048, 2048], P('tensor', ('dp', 'ctx'))
- grad_feedforward_gain: float32 [2048], P(('dp', 'ctx'))
- grad_gate_weight: float32 [2048, 5632], P(('dp', 'ctx'), 'tensor')
- grad_up_weight: float32 [2048, 5632], P(('dp', 'ctx'), 'tensor')
- grad_down_weight: float32 [5632, 2048], P('tensor', ('dp', 'ctx'))
Inputs may be any that keep to these rules, and one draw needn't show every extreme that they name: `segment_ids`: along each sequence the numbers start at 0 and rise by at most one from token to token over the documents; the last 1 to 128 tokens of every sequence are padding, marked -1. In every draw the first sequence holds documents of one token each and a single padding token.
All inputs are finite; a program needn't handle non-finite values.
Results may differ from a plain program's by a relative error of at most 0.018.
Values may be sent and summed in bfloat16 or wider, within the bound.
A program may use at most 192 MiB of HBM per device.

v0:
```python
import functools
import math

import jax
import jax.numpy as jnp
from jax import lax
from jax.experimental import pallas as pl
from jax.experimental.pallas import tpu as pltpu
from jax.sharding import PartitionSpec as P

HEAD_DIM = 64


epsilon = 1e-05
rope_base = 10000.0
masked_score = -1e30


def positions_of(segment):
    token_index = jnp.arange(segment.shape[-1], dtype=jnp.int32)
    previous = jnp.concatenate([segment[..., :1] - 1, segment[..., :-1]], axis=-1)
    starts = jnp.where(segment != previous, token_index, 0)
    earlier = token_index[None, :] <= token_index[:, None]
    run_start = jnp.max(jnp.where(earlier, starts[..., None, :], 0), axis=-1)
    return token_index - run_start


MESH = pl.DeviceIdType.MESH
CHUNK = 16
HOP = 2
MIB = 1 << 20
FRONT_MIB, BACK_MIB = 62, 62


def rotary_tables(positions):
    half_dim = HEAD_DIM // 2
    frequency = rope_base ** (-2.0 * jnp.arange(half_dim, dtype=jnp.float32) / HEAD_DIM)
    angles = positions.astype(jnp.float32)[..., None] * frequency
    return (jnp.cos(angles), jnp.sin(angles))


def rotate(values, cosine, sine_table):
    half_dim = values.shape[-1] // 2
    first = values[..., :half_dim]
    second = values[..., half_dim:]
    return jnp.concatenate(
        [first * cosine - second * sine_table, second * cosine + first * sine_table], axis=-1
    )


def visible(query_seg, key_seg, first_row):
    query_pos = first_row + jnp.arange(query_seg.shape[0], dtype=jnp.int32)
    key_pos = jnp.arange(key_seg.shape[0], dtype=jnp.int32)
    same_doc = query_seg[:, None] == key_seg[None, :]
    causal = key_pos[None, :] <= query_pos[:, None]
    usable = (key_seg[None, :] >= 0) | (key_pos[None, :] == query_pos[:, None])
    return same_doc & causal & usable


def turned_dot(left, right):
    return lax.dot_general(
        left, right, (((1,), (1,)), ((), ())), preferred_element_type=jnp.float32
    )


def remote(src, dst, send, recv, **device):
    return pltpu.make_async_remote_copy(
        src_ref=src, dst_ref=dst, send_sem=send, recv_sem=recv, device_id=device, device_id_type=MESH
    )


class Line:
    def __init__(self, line_size, own, finish, place, out_ref, held, acc_send, acc_recv, back_send, back_recv):
        self.last = line_size - 1
        self.here = lax.axis_index("tensor")
        self.own, self.finish, self.place = own, finish, place
        self.out_ref, self.held = out_ref, held
        self.acc_sems, self.back_sems = (acc_send, acc_recv), (back_send, back_recv)
        self.count = held.shape[1]

    def parts(self, stream):
        if stream == 0:
            return self.here, self.here + 1, self.here - 1
        return self.last - self.here, self.here - 1, self.here + 1

    def acc_copy(self, stream, i, target):
        ref = self.held.at[stream, i]
        return remote(ref, ref, self.acc_sems[0].at[stream, i], self.acc_sems[1].at[stream, i], tensor=target)

    def rows_of(self, stream, i):
        return pl.ds(pl.multiple_of(self.place(stream, i), CHUNK), CHUNK)

    def back_copy(self, stream, i, target):
        ref = self.out_ref.at[self.rows_of(stream, i)]
        return remote(ref, ref, self.back_sems[0].at[stream, i], self.back_sems[1].at[stream, i], tensor=target)

    def step(self, k, begin=0, size=None):
        last, held = self.last, self.held
        size = self.count if size is None else size
        for stream in (0, 1):
            place, after, before = self.parts(stream)
            due = k - HOP * place
            inside = (due >= 0) & (due < size)
            i = begin + due

            @pl.when(inside & (place == 0))
            def _():
                held[stream, i] = self.own(stream, i).astype(jnp.bfloat16)
                self.acc_copy(stream, i, after).start()

            @pl.when(inside & (place > 0) & (place < last))
            def _():
                self.acc_copy(stream, i, after).wait_recv()
                held[stream, i] = (held[stream, i].astype(jnp.float32) + self.own(stream, i)).astype(jnp.bfloat16)
                self.acc_copy(stream, i, after).start()

            @pl.when(inside & (place == last))
            def _():
                self.acc_copy(stream, i, before).wait_recv()
                total = held[stream, i].astype(jnp.float32) + self.own(stream, i)
                self.out_ref[self.rows_of(stream, i)] = self.finish(stream, i, total).astype(jnp.bfloat16)
                self.back_copy(stream, i, before).start()

            back = k - HOP * (2 * last - place)
            j = begin + back

            @pl.when((back >= 0) & (back < size) & (place < last))
            def _():
                self.back_copy(stream, j, before).wait_recv()

                @pl.when(place > 0)
                def _():
                    self.back_copy(stream, j, before).start()

    def drain(self):
        def sent(i, carry):
            for stream in (0, 1):
                place, after, before = self.parts(stream)

                @pl.when(place < self.last)
                def _():
                    self.acc_copy(stream, i, after).wait_send()

                @pl.when(place > 0)
                def _():
                    self.back_copy(stream, i, before).wait_send()

            return carry

        lax.fori_loop(0, self.count, sent, 0)


def line_scratch(rows, width):
    count = rows // 2 // CHUNK
    return [
        pltpu.VMEM((2, count, CHUNK, width), jnp.bfloat16),
        *[pltpu.SemaphoreType.DMA((2, count))] * 4,
    ]


def greet(line, core, plane, full_line=False):
    here, row, side = lax.axis_index("tensor"), lax.axis_index("dp"), lax.axis_index("ctx")
    barrier = pltpu.get_barrier_semaphore()
    peers = 0

    def call(**device):
        pl.semaphore_signal(barrier, inc=1, device_id=device, device_id_type=MESH)

    if full_line:
        for hop in range(1, line):
            call(tensor=lax.rem(here + hop, line))
        peers += line - 1
    else:

        @pl.when(here > 0)
        def _():
            call(tensor=here - 1)

        @pl.when(here < line - 1)
        def _():
            call(tensor=here + 1)

        peers = jnp.where(here > 0, 1, 0) + jnp.where(here < line - 1, 1, 0)
    if plane:
        for hop in range(1, 2 * plane):
            peer = lax.rem(2 * row + side + hop, 2 * plane)
            call(dp=peer // 2, ctx=lax.rem(peer, 2))
        peers += 2 * plane - 1
    elif core:
        call(ctx=1 - side)
        peers += 1
    pl.semaphore_wait(barrier, peers)


def kept_rows(i):
    return pl.ds(pl.multiple_of(i * CHUNK, CHUNK), CHUNK)


def rotate_lanes(values, cosine, signed_sine, back=False):
    lane = lax.broadcasted_iota(jnp.int32, values.shape, 1)
    swapped = jnp.where(
        lax.rem(lane, HEAD_DIM) < HEAD_DIM // 2,
        pltpu.roll(values, 128 - HEAD_DIM // 2, 1),
        pltpu.roll(values, HEAD_DIM // 2, 1),
    )
    turn = swapped * signed_sine
    return values * cosine - turn if back else values * cosine + turn


def key_lanes(values, turned):
    lane = lax.broadcasted_iota(jnp.int32, values.shape, 1)
    return jnp.where(lane < HEAD_DIM, turned, values)


def fill_bias(bias, seg_col, seg_row, first, keys, block):
    key_seg = seg_col[0:keys]
    query_seg = seg_row[:, first : first + block]
    key_pos = lax.broadcasted_iota(jnp.int32, (keys, block), 0)
    query_pos = first + lax.broadcasted_iota(jnp.int32, (keys, block), 1)
    usable = (key_seg >= 0) | (key_pos == query_pos)
    allowed = (key_seg == query_seg) & (key_pos <= query_pos) & usable
    bias[0:keys, :] = jnp.where(allowed, 0.0, masked_score)


def wide_tiles(width):
    return width // 256, width % 256


def inverse_rms(values):
    return lax.rsqrt(jnp.mean(values * values, axis=-1, keepdims=True) + epsilon)


def front_kernel(
    n, dp_size,
    inputs_any, segments, frequency, gain_one, gain_two,
    query_weight_any, key_weight_any, value_weight_any, out_weight_any, gate_weight_any, up_weight_any, down_weight_any, upstream_any,
    seg_out, cosine_out, sine_out, query_out, kv_out, log_out, mixed_out, normed_out, normed_two_out, up_out, inner_out, second_out,
    attended_out, middle_out, grad_middle_out, land_gate, gain_out, own_gate,
    seg_all, seg_row, seg_col, cosine, signed_sine,
    inputs, normed, query_weight, kv_weight, out_weight, query, kv, kv_turned, logs, mixed, bias,
    gate_weight, up_weight, down_weight, upstream, grad_inner, normed_two, gate, up, inner,
    partial, middle, grad_middle, two_other, turned, send_gate,
    load_sems, store_sems, core_send, core_recv, plane_send, plane_recv, *line_refs,
):
    span, width = inputs.shape
    hidden, piece = gate.shape[1], turned.shape[0]
    row, core = lax.axis_index("dp"), lax.axis_index("ctx")
    half, block = span // 2, span // 4
    second, attended = normed, inputs
    line_one, line_two = line_refs[:5], line_refs[5:]
    count = line_one[0].shape[1]
    part = count // 2

    def load(at, src, dst):
        made = pltpu.make_async_copy(src, dst, load_sems.at[at])
        made.start()
        return made

    def ordered(stream, i):
        return (i // part) * half + stream * block + lax.rem(i, part) * CHUNK

    def moved(at):
        return (0, 2, 1, 3)[at] * block

    load_inputs = load(0, inputs_any, inputs)
    load_query = load(1, query_weight_any, query_weight)
    load_kv = [
        load(2, key_weight_any, kv_weight.at[pl.ds(0, HEAD_DIM)]),
        load(11, value_weight_any, kv_weight.at[pl.ds(HEAD_DIM, HEAD_DIM)]),
    ]
    load_out = load(3, out_weight_any, out_weight)
    load_up = [
        load(4 + b, upstream_any.at[pl.ds(b * block, block)], upstream.at[pl.ds(moved(b), block)]) for b in range(4)
    ]
    load_down = load(8, down_weight_any, down_weight)
    load_gate = load(9, gate_weight_any, gate_weight)
    load_up_weight = load(10, up_weight_any, up_weight)
    seg_all[core] = jnp.broadcast_to(segments[...], seg_all.shape[1:])
    greet(n, True, dp_size)

    def seg_copy():
        return remote(seg_all.at[core], seg_all.at[core], core_send.at[1], core_recv.at[1], ctx=1 - core)

    seg_copy().start()
    load_inputs.wait()

    def norm_rows(b, carry):
        rows = pl.ds(pl.multiple_of(b * 64, 64), 64)
        value = inputs[rows].astype(jnp.float32)
        normed[rows] = (value * inverse_rms(value) * gain_one[...]).astype(jnp.bfloat16)
        return carry

    lax.fori_loop(0, span // 64, norm_rows, 0)
    seg_copy().wait()
    for side in (0, 1):
        seg_row[:, side * span : (side + 1) * span] = seg_all[side, 0:1]
        seg_col[side * span : (side + 1) * span] = seg_all[side].T[:, 0:1]
    own_seg = seg_all[core, 0:1]
    key_pos = lax.broadcasted_iota(jnp.int32, (2 * span, span), 0)
    query_pos = core * span + lax.broadcasted_iota(jnp.int32, (2 * span, span), 1)
    before = (seg_col[...] == own_seg) & (key_pos < query_pos)
    position = jnp.sum(jnp.where(before, 1.0, 0.0), axis=0, keepdims=True)
    angles = jnp.broadcast_to(position, (8, span)).T[:, 0:1] * frequency[...]
    lane = lax.broadcasted_iota(jnp.int32, angles.shape, 1)
    cosine[...] = jnp.cos(angles)
    sine = jnp.sin(angles)
    signed_sine[...] = jnp.where(lax.rem(lane, HEAD_DIM) < HEAD_DIM // 2, -sine, sine)
    for made in load_kv:
        made.wait()
    own_rows = pl.ds(pl.multiple_of(core * span, span), span)
    raw = turned_dot(normed[...], kv_weight[...])
    kv[own_rows] = key_lanes(raw, rotate_lanes(raw, cosine[...], signed_sine[...])).astype(jnp.bfloat16)

    def kv_copy():
        return remote(kv.at[own_rows], kv.at[own_rows], core_send.at[0], core_recv.at[0], ctx=1 - core)

    def kv_arrival():
        rows = pl.ds(0, span)
        return remote(kv.at[rows], kv.at[rows], core_send.at[0], core_recv.at[0], ctx=1 - core)

    @pl.when(core == 0)
    def _():
        kv_copy().start()

    load_query.wait()
    for low in range(0, span, half):
        rows = slice(low, low + half)
        raw = jnp.dot(normed[rows], query_weight[...], preferred_element_type=jnp.float32)
        for lanes in range(0, raw.shape[1], 128):
            rotated = rotate_lanes(raw[:, lanes : lanes + 128], cosine[rows], signed_sine[rows])
            query[rows, lanes : lanes + 128] = rotated.astype(jnp.bfloat16) * (HEAD_DIM ** -0.5)

    @pl.when(core == 1)
    def _():
        kv_arrival().wait_recv()

    kv_turned[...] = kv[...].T

    def attend(side, at):
        keys = side * span + (at + 1) * half
        rows = slice(at * half, (at + 1) * half)
        fill_bias(bias, seg_col, seg_row, side * span + at * half, keys, half)

        def pair(index, carry):
            lanes = pl.ds(pl.multiple_of(index * 128, 128), 128)
            both = query[rows, lanes]
            outs = []
            for which in (0, 1):
                scores = turned_dot(kv[0:keys, 0:HEAD_DIM], both[:, which * HEAD_DIM : (which + 1) * HEAD_DIM])
                scores = scores + bias[0:keys, :]
                peak = jnp.max(scores, axis=0, keepdims=True)
                grown = jnp.exp(scores - peak)
                total = jnp.sum(grown, axis=0, keepdims=True)
                logs[pl.ds(2 * index + which, 1), rows] = peak + jnp.log(total)
                out = jnp.dot(
                    kv_turned[HEAD_DIM : 2 * HEAD_DIM, 0:keys],
                    grown.astype(jnp.bfloat16),
                    preferred_element_type=jnp.float32,
                )
                outs.append(out / total)
            mixed[rows, lanes] = jnp.concatenate(outs, axis=0).T.astype(jnp.bfloat16)
            return carry

        lax.fori_loop(0, query.shape[1] // 128, pair, 0)

    for side in (0, 1):

        @pl.when(core == side)
        def _():
            attend(side, 0)
            attend(side, 1)

    load_out.wait()

    def out_tile(t, carry):
        columns = pl.ds(pl.multiple_of(t * 512, 512), 512)
        for b in (0, 2):
            value = jnp.dot(
                mixed[b * block : (b + 2) * block], out_weight[:, columns], preferred_element_type=jnp.float32
            )
            partial[moved(b) : moved(b) + block, columns] = value[:block]
            partial[moved(b + 1) : moved(b + 1) + block, columns] = value[block:]
        return carry

    lax.fori_loop(0, width // 512, out_tile, 0)

    def rows_at(start):
        return pl.ds(pl.multiple_of(start, CHUNK), CHUNK)

    def own(stream, i):
        return partial[rows_at(ordered(stream, i))]

    def finish_one(stream, i, total):
        value = inputs[rows_at((stream * count + i) * CHUNK)].astype(jnp.float32) + total
        middle[kept_rows(i)] = value
        return value * inverse_rms(value) * gain_two[...]

    gain_out[...] = jnp.zeros_like(gain_out)

    def finish_two(stream, i, total):
        value = middle[kept_rows(i)]
        inverse = inverse_rms(value)
        unit = value * inverse
        gain_out[0:1, :] += jnp.sum(total * unit, axis=0, keepdims=True)
        scaled = total * gain_two[...]
        result = upstream[rows_at(ordered(stream, i))].astype(jnp.float32) + inverse * (
            scaled - unit * jnp.mean(scaled * unit, axis=-1, keepdims=True)
        )
        grad_middle[kept_rows(i)] = result
        return result

    first = Line(n, own, finish_one, ordered, normed_two, *line_one)
    then = Line(n, own, finish_two, ordered, attended, *line_two)
    tiles, rest = wide_tiles(hidden)
    tile_count = tiles + (1 if rest else 0)

    def each_tile(t, work):
        @pl.when(t < tiles)
        def _():
            work(pl.ds(pl.multiple_of(t * 256, 256), 256))

        if rest:

            @pl.when(t == tiles)
            def _():
                work(pl.ds(tiles * 256, rest))

    def inner_tile(columns):
        grad_inner[:, columns] = turned_dot(upstream[...], down_weight[columns, :])

    def forward_tile(rows, columns):
        gated = jnp.dot(normed_two[rows], gate_weight[:, columns], preferred_element_type=jnp.float32)
        upped = jnp.dot(normed_two[rows], up_weight[:, columns], preferred_element_type=jnp.float32)
        sig = jax.nn.sigmoid(gated)
        act = gated * sig
        grad = grad_inner[rows, columns]
        inner[rows, columns] = (act * upped).astype(jnp.bfloat16)
        up[rows, columns] = (grad * act).astype(jnp.bfloat16)
        gate[rows, columns] = (grad * upped * sig * (1.0 + gated * (1.0 - sig))).astype(jnp.bfloat16)

    def back_tile(rows, t):
        columns = pl.ds(pl.multiple_of(t * 512, 512), 512)
        partial[rows, columns] = turned_dot(gate[rows], gate_weight[columns, :]) + turned_dot(
            up[rows], up_weight[columns, :]
        )

    def second_tile(rows, t):
        columns = pl.ds(pl.multiple_of(t * 512, 512), 512)
        second[rows, columns] = jnp.dot(
            inner[rows], down_weight[:, columns], preferred_element_type=jnp.float32
        ).astype(jnp.bfloat16)

    last = n - 1
    trip = 2 * HOP * last
    each = 2
    forward_steps, back_steps = -(-tile_count // each), width // 1024
    work = forward_steps + back_steps
    base_one = part + trip
    base_two = max(count + trip, base_one + work + 1)
    steps = base_two + work + part + trip

    def store(at, src, dst):
        return pltpu.make_async_copy(src, dst, store_sems.at[at])

    def stores(at, src, dst):
        return [
            store(at + b, src.at[pl.ds(moved(b), block)], dst.at[pl.ds(b * block, block)]) for b in range(4)
        ]

    early = [
        store(0, query, query_out), store(1, kv, kv_out), store(2, logs, log_out), store(3, mixed, mixed_out),
        store(31, seg_row, seg_out), store(32, cosine, cosine_out),
        store(33, signed_sine, sine_out),
    ]
    hidden_stores = [(5, normed_two, normed_two_out), (13, up, up_out), (17, inner, inner_out)]

    def gate_swaps():
        made = [
            remote(
                gate.at[pl.ds(0, span)], gate.at[pl.ds(span, span)], core_send.at[2], core_recv.at[2], ctx=1 - core
            )
        ]
        for q in range(dp_size):
            columns = pl.ds(pl.multiple_of((2 * q + 1 - core) * piece, piece), piece)
            made.append(
                remote(
                    normed_two.at[:, columns], two_other.at[:, pl.ds(q * piece, piece)],
                    core_send.at[3 + q], core_recv.at[3 + q], ctx=1 - core,
                )
            )
        return made

    def peer_of(r):
        return lax.rem(row + 1 + r, dp_size)

    def gate_copy(r):
        return remote(send_gate.at[r], land_gate.at[r], plane_send.at[r], plane_recv.at[r], dp=peer_of(r))

    def gate_piece(r):
        peer = peer_of(r)
        columns = pl.ds(pl.multiple_of((2 * peer + core) * piece, piece), piece)
        turned[:, 0:span] = normed_two[:, columns].T
        turned[:, span : 2 * span] = two_other[:, pl.ds(pl.multiple_of(peer * piece, piece), piece)].T
        edges = [(low, min(low + 384, hidden)) for low in range(0, hidden, 384)]

        @pl.when(r < dp_size - 1)
        def _():
            for low, high in edges:
                send_gate[r, :, low:high] = jnp.dot(
                    turned[...], gate[:, low:high], preferred_element_type=jnp.float32
                ).astype(jnp.bfloat16)
            gate_copy(r).start()

        @pl.when(r == dp_size - 1)
        def _():
            for low, high in edges:
                own_gate[:, low:high] = jnp.dot(turned[...], gate[:, low:high], preferred_element_type=jnp.float32)

    keep_normed = store(4, normed, normed_out)
    for made in [*early, keep_normed]:
        made.start()

    def step(k, carry):
        first.step(k)
        then.step(k - (base_one + work), 0, part)
        then.step(k - (base_two + work), part, part)

        @pl.when(k == 0)
        def _():
            for made in load_up:
                made.wait()
            load_down.wait()
            load_gate.wait()
            load_up_weight.wait()

        @pl.when((k >= 1) & (k <= tile_count))
        def _():
            each_tile(k - 1, inner_tile)

        late = jnp.where(k >= base_two, 1, 0)
        phase = k - jnp.where(k >= base_two, base_two, base_one)
        rows = pl.ds(pl.multiple_of(late * half, half), half)

        @pl.when((phase >= 0) & (phase < forward_steps))
        def _():
            def tile(t, carry):
                each_tile(t, functools.partial(forward_tile, rows))
                return carry

            lax.fori_loop(phase * each, jnp.minimum((phase + 1) * each, tile_count), tile, 0)

        @pl.when((phase >= forward_steps) & (phase < work))
        def _():
            for t in (0, 1):
                back_tile(rows, 2 * (phase - forward_steps) + t)

        @pl.when(k == base_two + work)
        def _():
            for at, src, dst in hidden_stores:
                for made in stores(at, src, dst):
                    made.start()

        @pl.when(k == base_two + forward_steps)
        def _():
            for made in gate_swaps():
                made.start()

        @pl.when(k == base_two + work + 1)
        def _():
            keep_normed.wait()
            for made in gate_swaps():
                made.wait()

        gate_task = k - (base_two + work + 1)

        @pl.when((gate_task >= 0) & (gate_task < dp_size))
        def _():
            gate_piece(gate_task)

        after = gate_task - dp_size

        @pl.when((after >= 0) & (after < 4))
        def _():
            for low in (0, half):
                second_tile(pl.ds(low, half), after)

        return carry

    lax.fori_loop(0, steps, step, 0)
    late_stores = [
        *stores(21, second, second_out), *stores(25, attended, attended_out),
        store(29, middle, middle_out), store(30, grad_middle, grad_middle_out),
    ]
    for made in late_stores:
        made.start()
    first.drain()
    then.drain()

    @pl.when(core == 0)
    def _():
        kv_copy().wait_send()

    for r in range(dp_size - 1):
        gate_copy(r).wait()
    for made in [*early, *late_stores]:
        made.wait()
    for at, src, dst in hidden_stores:
        for made in stores(at, src, dst):
            made.wait()


def front_call(line_size, dp_size, operands):
    inputs = operands[0]
    query_weight, out_weight, gate_weight = operands[5], operands[8], operands[9]
    span, width = inputs.shape
    heads, hidden = query_weight.shape[1], gate_weight.shape[1]
    piece = width // (2 * dp_size)
    low, full = jnp.bfloat16, jnp.float32
    vmem, outside = pl.BlockSpec(memory_space=pltpu.VMEM), pl.BlockSpec(memory_space=pl.ANY)
    dma = pltpu.SemaphoreType.DMA
    outs = [
        ((1, 2 * span), jnp.int32), ((span, 128), full), ((span, 128), full),
        ((span, heads), low), ((2 * span, 128), low), ((heads // HEAD_DIM, span), full), ((span, heads), low),
        ((span, width), low), ((span, width), low), *[((span, hidden), low)] * 2, ((span, width), low),
        ((span, width), low), ((span // 2, width), full), ((span // 2, width), full),
        ((dp_size - 1, piece, hidden), low), ((8, width), full), ((piece, hidden), full),
    ]
    scratch = [
        pltpu.VMEM((2, 8, span), jnp.int32), pltpu.VMEM((1, 2 * span), jnp.int32),
        pltpu.VMEM((2 * span, 1), jnp.int32), pltpu.VMEM((span, 128), full), pltpu.VMEM((span, 128), full),
        pltpu.VMEM((span, width), low), pltpu.VMEM((span, width), low), pltpu.VMEM((width, heads), low),
        pltpu.VMEM((128, width), low), pltpu.VMEM((heads, width), low), pltpu.VMEM((span, heads), low),
        pltpu.VMEM((2 * span, 128), low), pltpu.VMEM((128, 2 * span), low),
        pltpu.VMEM((heads // HEAD_DIM, span), full), pltpu.VMEM((span, heads), low),
        pltpu.VMEM((2 * span, span // 2), full),
        pltpu.VMEM((width, hidden), low), pltpu.VMEM((width, hidden), low), pltpu.VMEM((hidden, width), low),
        pltpu.VMEM((span, width), low), pltpu.VMEM((span, hidden), full), pltpu.VMEM((span, width), low),
        pltpu.VMEM((2 * span, hidden), low), *[pltpu.VMEM((span, hidden), low)] * 2,
        pltpu.VMEM((span, width), full),
        pltpu.VMEM((span // 2, width), full), pltpu.VMEM((span // 2, width), full),
        pltpu.VMEM((span, width // 2), low), pltpu.VMEM((piece, 2 * span), low),
        pltpu.VMEM((dp_size - 1, piece, hidden), low),
        dma((12,)), dma((34,)), dma((3 + dp_size,)), dma((3 + dp_size,)), dma((dp_size - 1,)), dma((dp_size - 1,)),
        *line_scratch(span, width), *line_scratch(span, width),
    ]
    return pl.pallas_call(
        functools.partial(front_kernel, line_size, dp_size),
        out_shape=[jax.ShapeDtypeStruct(s, d) for s, d in outs],
        in_specs=[outside] + [vmem] * 4 + [outside] * 8,
        out_specs=[outside] * 16 + [vmem] * 2,
        scratch_shapes=scratch,
        compiler_params=pltpu.CompilerParams(
            collective_id=1, has_side_effects=True, vmem_limit_bytes=FRONT_MIB * MIB
        ),
    )(*operands)


def back_kernel(
    n, dp_size,
    query_any, kv_any, logs, mixed_any, cosine, signed_sine, seg_row, inputs_any, normed_any, normed_two_any,
    up_any, inner_any, second_any, attended_any, middle_any, grad_middle_any, gain_one, gain_two_grad,
    query_weight_any, key_weight_any, value_weight_any, out_weight_any, upstream_any,
    layer_out, grad_inputs, grad_gains, grad_qkv, own_out, grad_up, own_down,
    land_up, land_down, land_qkv, land_out,
    query, kv, kv_turned, grad_mixed, mixed, attended, normed_cols, attended_cols, two_cols, upstream_cols,
    up, inner, pre, query_weight, kv_weight, out_weight, grad_middle, middle, inputs,
    ring, send_qkv, send_out, turned, seg_col, bias, kv_grad, kv_grad_other,
    gain_line, gain_land, gain_sum, gain_plane,
    load_sems, core_send, core_recv, ring_send, ring_recv, plane_send, plane_recv, line_send, line_recv,
    spread_send, spread_recv, *line_refs,
):
    span, width = attended.shape
    heads, piece = query.shape[1], turned.shape[0]
    here, row, core = lax.axis_index("tensor"), lax.axis_index("dp"), lax.axis_index("ctx")
    half = span // 2
    line_out, line_in = line_refs[:5], line_refs[5:]
    count = line_out[0].shape[1]
    last = n - 1
    loads = []

    def load(src, dst):
        made = pltpu.make_async_copy(src, dst, load_sems.at[len(loads)])
        made.start()
        loads.append(made)
        return made

    own_half = pl.ds(pl.multiple_of(jnp.where(here == 0, half, 0), half), half)
    first_loads = [
        load(second_any, layer_out), load(middle_any, middle),
        load(attended_any, attended), load(out_weight_any, out_weight), load(query_any, query), load(kv_any, kv),
    ]

    def load_cols(src, dst):
        made = []
        for q in range(dp_size):
            block = pl.multiple_of((2 * q + core) * piece, piece)
            made.append(load(src.at[:, pl.ds(block, piece)], dst.at[pl.ds(0, span), pl.ds(q * piece, piece)]))
        return made

    up_loads = [load(up_any, up.at[pl.ds(0, span)]), *load_cols(normed_two_any, two_cols)]
    inner_loads = [load(inner_any, inner.at[pl.ds(0, span)]), *load_cols(upstream_any, upstream_cols)]
    late_loads = [
        load(query_weight_any, query_weight), load(key_weight_any, kv_weight.at[pl.ds(0, HEAD_DIM)]),
        load(value_weight_any, kv_weight.at[pl.ds(HEAD_DIM, HEAD_DIM)]),
        load(grad_middle_any, grad_middle), load(inputs_any.at[own_half], inputs),
        load(mixed_any, mixed.at[pl.ds(0, span)]), *load_cols(normed_any, normed_cols),
        *load_cols(attended_any, attended_cols),
    ]
    greet(n, True, dp_size, full_line=True)
    slots = []

    def swap(src, dst):
        at = len(slots)
        slots.append(at)
        return remote(src, dst, core_send.at[at], core_recv.at[at], ctx=1 - core)

    def swap_rows(src, dst):
        return swap(src, dst.at[pl.ds(span, span)])

    def swap_cols(src, dst):
        made = []
        for q in range(dp_size):
            block = pl.multiple_of((2 * q + 1 - core) * piece, piece)
            made.append(
                swap(src.at[:, pl.ds(block, piece)], dst.at[pl.ds(span, span), pl.ds(q * piece, piece)])
            )
        return made

    up_swaps = [swap_rows(up_any, up), *swap_cols(normed_two_any, two_cols)]
    inner_swaps = [swap_rows(inner_any, inner), *swap_cols(upstream_any, upstream_cols)]
    late_swaps = [
        swap_rows(mixed_any, mixed), *swap_cols(attended_any, attended_cols), *swap_cols(normed_any, normed_cols),
    ]
    for made in [*up_swaps, *inner_swaps, *late_swaps]:
        made.start()
    pre_slot, kv_slot = len(slots), len(slots) + 1

    def pre_swap():
        return remote(
            pre.at[pl.ds(0, span)], pre.at[pl.ds(span, span)], core_send.at[pre_slot], core_recv.at[pre_slot],
            ctx=1 - core,
        )

    def kv_swap():
        return remote(
            kv_grad.at[pl.ds(0, span)], kv_grad_other, core_send.at[kv_slot], core_recv.at[kv_slot], ctx=1 - core
        )

    gain_line[...] = jnp.zeros_like(gain_line)
    gain_line[1:2, :] = gain_two_grad[0:1, :]
    kv_grad[...] = jnp.zeros_like(kv_grad)
    seg_col[...] = jnp.broadcast_to(seg_row[...], (8, 2 * span)).T[:, 0:1]
    for made in first_loads:
        made.wait()
    kv_turned[...] = kv[...].T

    def rows_at(start):
        return pl.ds(pl.multiple_of(start, CHUNK), CHUNK)

    def plain(stream, i):
        return (stream * count + i) * CHUNK

    def finish_out(stream, i, total):
        return middle[kept_rows(i)] + total

    def finish_in(stream, i, total):
        hidden = inputs[kept_rows(i)].astype(jnp.float32)
        inverse = inverse_rms(hidden)
        unit = hidden * inverse
        gain_line[0:1, :] += jnp.sum(total * unit, axis=0, keepdims=True)
        scaled = total * gain_one[...]
        return grad_middle[kept_rows(i)] + inverse * (
            scaled - unit * jnp.mean(scaled * unit, axis=-1, keepdims=True)
        )

    out_line = Line(
        n, lambda s, i: layer_out[rows_at(plain(s, i))].astype(jnp.float32), finish_out, plain, layer_out, *line_out
    )
    in_line = Line(
        n, lambda s, i: grad_inputs[rows_at(plain(s, i))].astype(jnp.float32), finish_in, plain, grad_inputs, *line_in
    )

    def attend_back(side, at, index):
        keys = side * span + (at + 1) * half
        rows = slice(at * half, (at + 1) * half)
        lanes = pl.ds(pl.multiple_of(index * 128, 128), 128)

        @pl.when(index == 0)
        def _():
            fill_bias(bias, seg_col, seg_row, side * span + at * half, keys, half)

        both_query, both_grad = query[rows, lanes], grad_mixed[rows, lanes]
        outs, parts = [], None
        for which in (0, 1):
            head = slice(which * HEAD_DIM, (which + 1) * HEAD_DIM)
            query_head, grad_head = both_query[:, head], both_grad[:, head]
            scores = turned_dot(kv[0:keys, 0:HEAD_DIM], query_head) + bias[0:keys, :]
            probs = jnp.exp(scores - logs[pl.ds(2 * index + which, 1), rows])
            grad_probs = turned_dot(kv[0:keys, HEAD_DIM : 2 * HEAD_DIM], grad_head)
            both = probs * grad_probs
            grad_scores = (both - probs * jnp.sum(both, axis=0, keepdims=True)).astype(jnp.bfloat16)
            grad_key = jnp.dot(grad_scores, query_head, preferred_element_type=jnp.float32)
            grad_value = jnp.dot(probs.astype(jnp.bfloat16), grad_head, preferred_element_type=jnp.float32)
            part = jnp.concatenate([grad_key, grad_value], axis=1)
            parts = part if parts is None else parts + part
            outs.append(
                jnp.dot(kv_turned[0:HEAD_DIM, 0:keys], grad_scores, preferred_element_type=jnp.float32)
            )
        kv_grad[0:keys] += parts
        grad_query = jnp.concatenate(outs, axis=0).T * (HEAD_DIM ** -0.5)
        pre[rows, lanes] = rotate_lanes(grad_query, cosine[rows], signed_sine[rows], back=True).astype(jnp.bfloat16)

    pairs = heads // 128
    tasks = 2 * pairs

    def attend_task(task):
        for side in (0, 1):
            for at in (0, 1):

                @pl.when((core == side) & (task // pairs == at))
                def _():
                    attend_back(side, at, lax.rem(task, pairs))

    own_grad = pl.ds(pl.multiple_of(core * span, span), span)

    def finish_pre():
        @pl.when(core == 0)
        def _():
            kv_swap().wait_recv()
            kv_grad[0:span] += kv_grad_other[...]

        raw = kv_grad[own_grad]
        turned_back = rotate_lanes(raw, cosine[...], signed_sine[...], back=True)
        pre[0:span, heads : heads + 128] = key_lanes(raw, turned_back).astype(jnp.bfloat16)

    def in_products():
        def tile(t, carry):
            columns = pl.ds(pl.multiple_of(t * 512, 512), 512)
            for low in (0, half):
                rows = slice(low, low + half)
                grad_inputs[rows, columns] = (
                    turned_dot(pre[rows, 0:heads], query_weight[columns, :])
                    + jnp.dot(
                        pre[rows, heads : heads + 128], kv_weight[:, columns], preferred_element_type=jnp.float32
                    )
                ).astype(jnp.bfloat16)
            return carry

        lax.fori_loop(0, width // 512, tile, 0)

    def peer_of(r):
        return lax.rem(row + 1 + r, dp_size)

    def turn(r, cols):
        block = pl.multiple_of(peer_of(r) * piece, piece)
        turned[...] = cols[:, pl.ds(block, piece)].T

    def tiles_of(stacked):
        wide = stacked.shape[1]
        return [(low, min(low + 384, wide)) for low in range(0, wide, 384)]

    def piece_value(stacked, low, high):
        return jnp.dot(turned[...], stacked[:, low:high], preferred_element_type=jnp.float32)

    landings = (land_up, land_down)
    others = dp_size - 1

    def ring_copy(w, r, at):
        return remote(
            ring.at[at], landings[w].at[r], ring_send.at[at], ring_recv.at[w, r], dp=peer_of(r)
        )

    def ring_piece(w, r, stacked, own):
        at = others * w + r

        @pl.when(r < dp_size - 1)
        def _():
            slot = at

            for low, high in tiles_of(stacked):
                ring[slot, :, low:high] = piece_value(stacked, low, high).astype(jnp.bfloat16)
            ring_copy(w, r, at).start()

        @pl.when(r == dp_size - 1)
        def _():
            for low, high in tiles_of(stacked):
                own[:, low:high] = piece_value(stacked, low, high)

    sends, lands = (send_qkv, send_out), (land_qkv, land_out)

    def plane_copy(w, r):
        return remote(sends[w].at[r], lands[w].at[r], plane_send.at[w, r], plane_recv.at[w, r], dp=peer_of(r))

    def plane_piece(w, r, stacked, own):
        @pl.when(r < dp_size - 1)
        def _():
            for low, high in tiles_of(stacked):
                sends[w][r, :, low:high] = piece_value(stacked, low, high).astype(jnp.bfloat16)
            plane_copy(w, r).start()

        @pl.when(r == dp_size - 1)
        def _():
            for low, high in tiles_of(stacked):
                own[:, low:high] = piece_value(stacked, low, high)

    def line_copies(owner, hops):
        slot = 0 if owner == 0 else 1
        return [
            remote(
                gain_line, gain_land.at[slot], line_send.at[slot, hop - 1], line_recv.at[slot],
                tensor=owner + hop if owner == 0 else owner - hop,
            )
            for hop in hops
        ]

    lag = tasks + 2
    ffn_tasks = 2 * dp_size
    out_base = max(ffn_tasks + 1, lag + 1)
    steps = max(lag + count + 2 * HOP * last, out_base + dp_size)

    def step(k, carry):
        out_line.step(k)
        in_line.step(k - lag)

        @pl.when(k == 0)
        def _():
            grad_mixed[...] = turned_dot(attended[...], out_weight[...]).astype(jnp.bfloat16)

        @pl.when((k >= 1) & (k <= tasks))
        def _():
            attend_task(k - 1)

        @pl.when((k == tasks) & (core == 1))
        def _():
            kv_swap().start()

        @pl.when(k == 1)
        def _():
            for made in [*up_loads, *up_swaps]:
                made.wait()

        @pl.when(k == dp_size + 1)
        def _():
            for made in [*inner_loads, *inner_swaps]:
                made.wait()

        @pl.when(k == tasks)
        def _():
            for made in late_loads:
                made.wait()
            for made in late_swaps:
                made.wait()

        @pl.when(k == tasks + 1)
        def _():
            finish_pre()
            in_products()
            pre_swap().start()

        r = k - 1

        @pl.when((r >= 0) & (r < dp_size))
        def _():
            turn(r, two_cols)
            ring_piece(0, r, up, grad_up)

        @pl.when((r >= dp_size) & (r < 2 * dp_size))
        def _():
            turn(r - dp_size, upstream_cols)
            ring_piece(1, r - dp_size, inner, own_down)

        @pl.when(k == out_base)
        def _():
            pre_swap().wait()

        at = k - out_base

        @pl.when((at >= 0) & (at < dp_size))
        def _():
            turn(at, attended_cols)
            plane_piece(1, at, mixed, own_out)
            turn(at, normed_cols)
            plane_piece(0, at, pre, grad_qkv)

        @pl.when(k == lag + count + HOP * last - 1)
        def _():
            for owner in (0, last):

                @pl.when(here == owner)
                def _():
                    for made in line_copies(owner, range(1, n)):
                        made.start()

        return carry

    lax.fori_loop(0, steps, step, 0)
    shard = width // (2 * dp_size)
    gain_sum[...] = jnp.zeros_like(gain_sum)
    for owner in (0, last):
        slot = 0 if owner == 0 else 1

        @pl.when(here == owner)
        def _():
            gain_sum[...] += gain_line[...]

        @pl.when(here != owner)
        def _():
            line_copies(owner, (1,))[0].wait_recv()
            gain_sum[...] += gain_land[slot]

    shards = 2 * dp_size
    place = 2 * row + core

    def spread(r):
        peer = lax.rem(place + 1 + r, shards)
        block = pl.multiple_of(peer * shard, shard)
        return remote(
            gain_sum.at[:, pl.ds(block, shard)], gain_plane.at[r], spread_send.at[r], spread_recv.at[r],
            dp=peer // 2, ctx=lax.rem(peer, 2),
        )

    for r in range(shards - 1):
        spread(r).start()
    out_line.drain()
    in_line.drain()

    @pl.when(core == 1)
    def _():
        kv_swap().wait_send()

    for r in range(others):
        for w in (0, 1):
            ring_copy(w, r, others * w + r).wait()
            plane_copy(w, r).wait()
    grad_gains[...] = gain_sum[:, pl.ds(pl.multiple_of(place * shard, shard), shard)]
    for r in range(shards - 1):
        spread(r).wait()
        grad_gains[...] += gain_plane[r]
    for owner in (0, last):

        @pl.when(here == owner)
        def _():
            for made in line_copies(owner, range(1, n)):
                made.wait_send()


def back_call(line_size, dp_size, operands):
    query, kv, logs, mixed = operands[:4]
    span, heads = query.shape
    width, hidden = operands[8].shape[1], operands[10].shape[1]
    piece = width // (2 * dp_size)
    wide = heads + 128
    low, full = jnp.bfloat16, jnp.float32
    vmem, outside = pl.BlockSpec(memory_space=pltpu.VMEM), pl.BlockSpec(memory_space=pl.ANY)
    dma = pltpu.SemaphoreType.DMA
    others = dp_size - 1
    outs = [
        ((span, width), low), ((span, width), low), ((8, piece), full), ((piece, wide), full), ((piece, heads), full),
        ((piece, hidden), full), ((piece, hidden), full),
        *[((others, piece, hidden), low)] * 2, ((others, piece, wide), low), ((others, piece, heads), low),
    ]
    core_copies = 3 + 4 * dp_size + 2
    scratch = [
        pltpu.VMEM((span, heads), low), pltpu.VMEM((2 * span, 128), low), pltpu.VMEM((128, 2 * span), low),
        pltpu.VMEM((span, heads), low), pltpu.VMEM((2 * span, heads), low), pltpu.VMEM((span, width), low),
        *[pltpu.VMEM((2 * span, width // 2), low)] * 4,
        *[pltpu.VMEM((2 * span, hidden), low)] * 2, pltpu.VMEM((2 * span, wide), low),
        pltpu.VMEM((width, heads), low), pltpu.VMEM((128, width), low), pltpu.VMEM((heads, width), low),
        pltpu.VMEM((span // 2, width), full), pltpu.VMEM((span // 2, width), full), pltpu.VMEM((span // 2, width), low),
        pltpu.VMEM((2 * others, piece, hidden), low), pltpu.VMEM((others, piece, wide), low),
        pltpu.VMEM((others, piece, heads), low),
        pltpu.VMEM((piece, 2 * span), low), pltpu.VMEM((2 * span, 1), jnp.int32), pltpu.VMEM((2 * span, span // 2), full),
        pltpu.VMEM((2 * span, 128), full), pltpu.VMEM((span, 128), full),
        pltpu.VMEM((8, width), full), pltpu.VMEM((2, 8, width), full), pltpu.VMEM((8, width), full),
        pltpu.VMEM((2 * dp_size - 1, 8, piece), full),
        dma((17 + 4 * dp_size + 6,)), dma((core_copies,)), dma((core_copies,)),
        dma((2 * others,)), dma((2, others)), dma((2, others)), dma((2, others)),
        dma((2, line_size - 1)), dma((2,)), dma((2 * dp_size - 1,)), dma((2 * dp_size - 1,)),
        *line_scratch(span, width), *line_scratch(span, width),
    ]
    spaces = [outside, outside, vmem, outside, vmem, vmem, vmem] + [outside] * 9 + [vmem, vmem] + [outside] * 5
    return pl.pallas_call(
        functools.partial(back_kernel, line_size, dp_size),
        out_shape=[jax.ShapeDtypeStruct(s, d) for s, d in outs],
        in_specs=spaces,
        out_specs=[vmem] * 7 + [outside] * 4,
        scratch_shapes=scratch,
        compiler_params=pltpu.CompilerParams(
            collective_id=2, has_side_effects=True, vmem_limit_bytes=BACK_MIB * MIB
        ),
    )(*operands)


def settle_kernel(
    layer_any, inputs_any, gains, qkv_any, out_any, gate_any, up_any, down_any,
    land_gate, land_up, land_down, land_qkv, land_out,
    layer_out, grad_inputs, gain_one, grad_query, grad_key, grad_value, grad_out, gain_two, grad_gate, grad_up, grad_down,
    own_qkv, own_out, own_gate, own_up, own_down, far_qkv, far_out, far_gate, far_up, far_down,
    turned_kv, turned_out, turned_down, in_sems, out_sems,
):
    whole = [
        pltpu.make_async_copy(layer_any, layer_out, out_sems.at[0]),
        pltpu.make_async_copy(inputs_any, grad_inputs, out_sems.at[1]),
    ]
    owns = ((qkv_any, own_qkv), (out_any, own_out), (gate_any, own_gate), (up_any, own_up), (down_any, own_down))
    fars = ((land_qkv, far_qkv), (land_out, far_out), (land_gate, far_gate), (land_up, far_up), (land_down, far_down))
    loads = [
        (
            pltpu.make_async_copy(*own, in_sems.at[0, at]),
            pltpu.make_async_copy(*far, in_sems.at[1, at]),
        )
        for at, (own, far) in enumerate(zip(owns, fars))
    ]
    for pair in loads:
        for made in pair:
            made.start()
    for made in whole:
        made.start()
    gain_one[...] = gains[0:1]
    gain_two[...] = gains[1:2]

    def settle(at, own, far):
        for made in loads[at]:
            made.wait()
        total = own[...]
        for r in range(far.shape[0]):
            total = total + far[r].astype(jnp.float32)
        return total

    def put(at, src, dst):
        made = pltpu.make_async_copy(src, dst, out_sems.at[at])
        made.start()
        whole.append(made)

    heads = grad_query.shape[1]
    own_qkv[...] = settle(0, own_qkv, far_qkv)
    put(2, own_qkv.at[:, pl.ds(0, heads)], grad_query)
    turned_kv[...] = own_qkv[:, heads:].T
    put(3, turned_kv.at[pl.ds(0, HEAD_DIM)], grad_key)
    put(4, turned_kv.at[pl.ds(HEAD_DIM, HEAD_DIM)], grad_value)
    turned_out[...] = settle(1, own_out, far_out).T
    put(5, turned_out, grad_out)
    own_gate[...] = settle(2, own_gate, far_gate)
    put(6, own_gate, grad_gate)
    own_up[...] = settle(3, own_up, far_up)
    put(7, own_up, grad_up)
    turned_down[...] = settle(4, own_down, far_down).T
    put(8, turned_down, grad_down)
    for made in whole:
        made.wait()


def settle_call(operands):
    layer_out, _, gains, qkv, out, gate = operands[:6]
    piece, wide = qkv.shape
    heads, hidden = out.shape[1], gate.shape[1]
    others = operands[8].shape[0]
    low, full = jnp.bfloat16, jnp.float32
    vmem, outside = pl.BlockSpec(memory_space=pltpu.VMEM), pl.BlockSpec(memory_space=pl.ANY)
    outs = [
        (layer_out.shape, low), (layer_out.shape, low), ((1, piece), full), ((piece, heads), full),
        ((HEAD_DIM, piece), full), ((HEAD_DIM, piece), full), ((heads, piece), full), ((1, piece), full),
        ((piece, hidden), full), ((piece, hidden), full), ((hidden, piece), full),
    ]
    shapes = [(piece, wide), (piece, heads), *[(piece, hidden)] * 3]
    scratch = [
        *[pltpu.VMEM(shape, full) for shape in shapes], *[pltpu.VMEM((others, *shape), low) for shape in shapes],
        pltpu.VMEM((wide - heads, piece), full), pltpu.VMEM((heads, piece), full), pltpu.VMEM((hidden, piece), full),
        pltpu.SemaphoreType.DMA((2, 5)), pltpu.SemaphoreType.DMA((9,)),
    ]
    return pl.pallas_call(
        settle_kernel,
        out_shape=[jax.ShapeDtypeStruct(s, d) for s, d in outs],
        in_specs=[outside, outside, vmem] + [outside] * 10,
        out_specs=[outside, outside, vmem] + [outside] * 4 + [vmem] + [outside] * 3,
        scratch_shapes=scratch,
        compiler_params=pltpu.CompilerParams(vmem_limit_bytes=40 * MIB),
    )(*operands)


def plain_body(
    inputs,
    segment_ids,
    attention_gain,
    query_weight,
    key_weight,
    value_weight,
    out_weight,
    feedforward_gain,
    gate_weight,
    up_weight,
    down_weight,
    cotangent,
):
    seq_count, span_len, model_width = inputs.shape
    row_count = seq_count * span_len
    query_heads = query_weight.shape[1] // HEAD_DIM
    kv_heads = key_weight.shape[1] // HEAD_DIM
    group_size = query_heads // kv_heads
    score_scale = 1.0 / math.sqrt(HEAD_DIM)
    offset = lax.axis_index("ctx") * span_len
    whole_segments = lax.all_gather(segment_ids, "ctx", axis=1, tiled=True)
    own_positions = lax.dynamic_slice_in_dim(positions_of(whole_segments), offset, span_len, 1)
    cosine, sine_table = rotary_tables(own_positions)
    cosine = cosine[:, :, None, :]
    sine_table = sine_table[:, :, None, :]
    hidden = inputs.astype(jnp.float32).reshape(row_count, model_width)
    inverse_one = lax.rsqrt(jnp.mean(hidden * hidden, axis=-1, keepdims=True) + epsilon)
    unit_one = hidden * inverse_one
    normed = (unit_one * attention_gain).astype(jnp.bfloat16)
    query_rows = rotate(
        jnp.dot(normed, query_weight, preferred_element_type=jnp.float32).reshape(
            seq_count, span_len, query_heads, HEAD_DIM
        ),
        cosine,
        sine_table,
    ).astype(jnp.bfloat16)
    key_rows = rotate(
        jnp.dot(normed, key_weight, preferred_element_type=jnp.float32).reshape(
            seq_count, span_len, kv_heads, HEAD_DIM
        ),
        cosine,
        sine_table,
    ).astype(jnp.bfloat16)
    value_rows = (
        jnp.dot(normed, value_weight, preferred_element_type=jnp.float32)
        .astype(jnp.bfloat16)
        .reshape(seq_count, span_len, kv_heads, HEAD_DIM)
    )
    all_keys, all_values = (
        lax.all_gather(key_rows, "ctx", axis=1, tiled=True),
        lax.all_gather(value_rows, "ctx", axis=1, tiled=True),
    )

    def attend(block_items):
        query_block, key_block, value_block, query_seg, key_seg = block_items
        allowed = visible(query_seg, key_seg, offset)
        grouped = query_block.reshape(span_len, kv_heads, group_size, HEAD_DIM)
        raw_scores = jnp.einsum(
            "qhgd,khd->hgqk", grouped, key_block, preferred_element_type=jnp.float32
        )
        scores = jnp.where(allowed, raw_scores * score_scale, masked_score)
        row_peak = jnp.max(scores, axis=-1, keepdims=True)
        shifted_exp = jnp.exp(scores - row_peak)
        denominator = jnp.sum(shifted_exp, axis=-1, keepdims=True)
        attn_probs = (shifted_exp / denominator).astype(jnp.bfloat16)
        mixed_block = jnp.einsum(
            "hgqk,khd->qhgd", attn_probs, value_block, preferred_element_type=jnp.float32
        )
        return (
            mixed_block.astype(jnp.bfloat16).reshape(span_len, query_heads * HEAD_DIM),
            row_peak + jnp.log(denominator),
        )

    mixed_heads, log_sums = lax.map(
        attend, (query_rows, all_keys, all_values, segment_ids, whole_segments)
    )
    mixed_flat = mixed_heads.reshape(row_count, query_heads * HEAD_DIM)
    attended = lax.psum(
        jnp.dot(mixed_flat, out_weight, preferred_element_type=jnp.float32), "tensor"
    )
    middle = hidden + attended
    inverse_two = lax.rsqrt(jnp.mean(middle * middle, axis=-1, keepdims=True) + epsilon)
    unit_two = middle * inverse_two
    normed_two = (unit_two * feedforward_gain).astype(jnp.bfloat16)
    gate_pre = jnp.dot(normed_two, gate_weight, preferred_element_type=jnp.float32)
    up_pre = jnp.dot(normed_two, up_weight, preferred_element_type=jnp.float32)
    sigmoid_gate = jax.nn.sigmoid(gate_pre)
    inner_act = (gate_pre * sigmoid_gate * up_pre).astype(jnp.bfloat16)
    feed_out = lax.psum(
        jnp.dot(inner_act, down_weight, preferred_element_type=jnp.float32).astype(jnp.bfloat16),
        "tensor",
    ).astype(jnp.float32)
    layer_out = (middle + feed_out).astype(jnp.bfloat16).reshape(seq_count, span_len, model_width)
    upstream = cotangent.reshape(row_count, model_width)
    grad_down = jnp.dot(inner_act.T, upstream, preferred_element_type=jnp.float32)
    grad_inner = jnp.dot(upstream, down_weight.T, preferred_element_type=jnp.float32)
    grad_up_pre = (grad_inner * gate_pre * sigmoid_gate).astype(jnp.bfloat16)
    grad_gate_pre = (
        grad_inner * up_pre * sigmoid_gate * (1.0 + gate_pre * (1.0 - sigmoid_gate))
    ).astype(jnp.bfloat16)
    grad_gate = jnp.dot(normed_two.T, grad_gate_pre, preferred_element_type=jnp.float32)
    grad_up = jnp.dot(normed_two.T, grad_up_pre, preferred_element_type=jnp.float32)
    grad_normed_two = lax.psum(
        jnp.dot(grad_gate_pre, gate_weight.T, preferred_element_type=jnp.float32)
        + jnp.dot(grad_up_pre, up_weight.T, preferred_element_type=jnp.float32),
        "tensor",
    )
    grad_ffn_gain = jnp.sum(grad_normed_two * unit_two, axis=0)
    scaled_two = grad_normed_two * feedforward_gain
    grad_middle = upstream.astype(jnp.float32) + inverse_two * (
        scaled_two - unit_two * jnp.mean(scaled_two * unit_two, axis=-1, keepdims=True)
    )
    grad_attended = grad_middle.astype(jnp.bfloat16)
    grad_out_part = jnp.dot(mixed_flat.T, grad_attended, preferred_element_type=jnp.float32)
    grad_mixed = (
        jnp.dot(grad_attended, out_weight.T, preferred_element_type=jnp.float32)
        .astype(jnp.bfloat16)
        .reshape(seq_count, span_len, query_heads, HEAD_DIM)
    )

    def attend_back(block_items):
        query_block, key_block, value_block, query_seg, key_seg, grad_block, log_block = block_items
        allowed = visible(query_seg, key_seg, offset)
        grouped = query_block.reshape(span_len, kv_heads, group_size, HEAD_DIM)
        grad_grouped = grad_block.reshape(span_len, kv_heads, group_size, HEAD_DIM)
        raw_scores = jnp.einsum(
            "qhgd,khd->hgqk", grouped, key_block, preferred_element_type=jnp.float32
        )
        scores = jnp.where(allowed, raw_scores * score_scale, masked_score)
        attn_probs = jnp.exp(scores - log_block)
        rounded = attn_probs.astype(jnp.bfloat16)
        grad_values = jnp.einsum(
            "hgqk,qhgd->khd", rounded, grad_grouped, preferred_element_type=jnp.float32
        )
        grad_probs = jnp.einsum(
            "qhgd,khd->hgqk", grad_grouped, value_block, preferred_element_type=jnp.float32
        )
        row_dot = jnp.sum(attn_probs * grad_probs, axis=-1, keepdims=True)
        grad_scores = (attn_probs * (grad_probs - row_dot) * score_scale).astype(jnp.bfloat16)
        grad_queries = jnp.einsum(
            "hgqk,khd->qhgd", grad_scores, key_block, preferred_element_type=jnp.float32
        ).reshape(span_len, query_heads, HEAD_DIM)
        grad_keys = jnp.einsum(
            "hgqk,qhgd->khd", grad_scores, grouped, preferred_element_type=jnp.float32
        )
        return (grad_queries, grad_keys, grad_values)

    grad_queries, grad_keys, grad_values = lax.map(
        attend_back,
        (query_rows, all_keys, all_values, segment_ids, whole_segments, grad_mixed, log_sums),
    )
    own_grad_keys, own_grad_values = (
        lax.psum_scatter(grad_keys, "ctx", scatter_dimension=1, tiled=True),
        lax.psum_scatter(grad_values, "ctx", scatter_dimension=1, tiled=True),
    )
    grad_query_pre = (
        rotate(grad_queries, cosine, -sine_table)
        .astype(jnp.bfloat16)
        .reshape(row_count, query_heads * HEAD_DIM)
    )
    grad_key_pre = (
        rotate(own_grad_keys, cosine, -sine_table)
        .astype(jnp.bfloat16)
        .reshape(row_count, kv_heads * HEAD_DIM)
    )
    grad_value_pre = own_grad_values.astype(jnp.bfloat16).reshape(row_count, kv_heads * HEAD_DIM)
    grad_query = jnp.dot(normed.T, grad_query_pre, preferred_element_type=jnp.float32)
    grad_key = jnp.dot(normed.T, grad_key_pre, preferred_element_type=jnp.float32)
    grad_value = jnp.dot(normed.T, grad_value_pre, preferred_element_type=jnp.float32)
    grad_normed = lax.psum(
        (
            jnp.dot(grad_query_pre, query_weight.T, preferred_element_type=jnp.float32)
            + jnp.dot(grad_key_pre, key_weight.T, preferred_element_type=jnp.float32)
            + jnp.dot(grad_value_pre, value_weight.T, preferred_element_type=jnp.float32)
        ).astype(jnp.bfloat16),
        "tensor",
    ).astype(jnp.float32)
    grad_attn_gain = jnp.sum(grad_normed * unit_one, axis=0)
    scaled_one = grad_normed * attention_gain
    grad_hidden = grad_middle + inverse_one * (
        scaled_one - unit_one * jnp.mean(scaled_one * unit_one, axis=-1, keepdims=True)
    )
    grad_inputs = grad_hidden.astype(jnp.bfloat16).reshape(seq_count, span_len, model_width)
    reduced = (
        lax.psum_scatter(
            grad_attn_gain.astype(jnp.bfloat16), ("dp", "ctx"), scatter_dimension=0, tiled=True
        ).astype(jnp.float32),
        lax.psum_scatter(
            grad_query.astype(jnp.bfloat16), ("dp", "ctx"), scatter_dimension=0, tiled=True
        ).astype(jnp.float32),
        lax.psum_scatter(
            grad_key.astype(jnp.bfloat16), ("dp", "ctx"), scatter_dimension=0, tiled=True
        ).astype(jnp.float32),
        lax.psum_scatter(
            grad_value.astype(jnp.bfloat16), ("dp", "ctx"), scatter_dimension=0, tiled=True
        ).astype(jnp.float32),
        lax.psum_scatter(
            grad_out_part.astype(jnp.bfloat16), ("dp", "ctx"), scatter_dimension=1, tiled=True
        ).astype(jnp.float32),
        lax.psum_scatter(
            grad_ffn_gain.astype(jnp.bfloat16), ("dp", "ctx"), scatter_dimension=0, tiled=True
        ).astype(jnp.float32),
        lax.psum_scatter(
            grad_gate.astype(jnp.bfloat16), ("dp", "ctx"), scatter_dimension=0, tiled=True
        ).astype(jnp.float32),
        lax.psum_scatter(
            grad_up.astype(jnp.bfloat16), ("dp", "ctx"), scatter_dimension=0, tiled=True
        ).astype(jnp.float32),
        lax.psum_scatter(
            grad_down.astype(jnp.bfloat16), ("dp", "ctx"), scatter_dimension=1, tiled=True
        ).astype(jnp.float32),
    )
    return (
        layer_out,
        grad_inputs,
        reduced[0],
        reduced[1],
        reduced[2],
        reduced[3],
        reduced[4],
        reduced[5],
        reduced[6],
        reduced[7],
        reduced[8],
    )


def fast_body(
    inputs, segment_ids, attention_gain, query_weight, key_weight, value_weight, out_weight, feedforward_gain,
    gate_weight, up_weight, down_weight, cotangent,
):
    _, span_len, model_width = inputs.shape
    line_size, dp_size = lax.axis_size("tensor"), lax.axis_size("dp")
    half_dim = HEAD_DIM // 2
    frequency = rope_base ** (-2.0 * jnp.arange(half_dim, dtype=jnp.float32) / HEAD_DIM)
    frequency = jnp.tile(frequency, 4).reshape(1, 128)
    flat_inputs = inputs.reshape(span_len, model_width)
    upstream = cotangent.reshape(span_len, model_width)
    gain_one, gain_two = attention_gain.reshape(1, -1), feedforward_gain.reshape(1, -1)
    key_turned, value_turned = key_weight.T, value_weight.T
    (
        seg_row, cosine, signed_sine, query, kv, logs, mixed, normed, normed_two, up, inner, second, attended,
        middle, grad_middle, land_gate, gain_grad, own_gate,
    ) = front_call(
        line_size, dp_size,
        (
            flat_inputs, segment_ids, frequency, gain_one, gain_two, query_weight, key_turned, value_turned, out_weight,
            gate_weight, up_weight, down_weight, upstream,
        ),
    )
    (
        layer_out, grad_inputs, gains, own_qkv, own_out, own_up, own_down, land_up, land_down, land_qkv, land_out
    ) = back_call(
        line_size, dp_size,
        (
            query, kv, logs, mixed, cosine, signed_sine, seg_row, flat_inputs, normed, normed_two,
            up, inner, second, attended, middle, grad_middle, gain_one, gain_grad,
            query_weight, key_turned, value_turned, out_weight, upstream,
        ),
    )
    layer_out, grad_inputs, gain_a, grad_query, grad_key, grad_value, grad_out, gain_b, *ffn = settle_call(
        (
            layer_out, grad_inputs, gains, own_qkv, own_out, own_gate, own_up, own_down,
            land_gate, land_up, land_down, land_qkv, land_out,
        )
    )
    shape = (1, span_len, model_width)
    return (
        layer_out.reshape(shape), grad_inputs.reshape(shape), gain_a[0], grad_query, grad_key.T, grad_value.T,
        grad_out, gain_b[0], *ffn,
    )


def body(mesh, *arrays):
    inputs = arrays[0]
    span_len, model_width = inputs.shape[1:]
    dp_size, ctx_size, line_size = mesh.shape["dp"], mesh.shape["ctx"], mesh.shape["tensor"]
    piece = model_width // (dp_size * ctx_size)
    fits = inputs.shape[0] == 1 and ctx_size == 2 and dp_size > 1 and line_size > 1
    if fits and piece % 128 == 0 and span_len % (2 * CHUNK) == 0:
        return fast_body(*arrays)
    return plain_body(*arrays)


def solution(mesh):
    return jax.shard_map(
        functools.partial(body, mesh),
        mesh=mesh,
        in_specs=(
            P("dp", "ctx", None),
            P("dp", "ctx"),
            P(),
            P(None, "tensor"),
            P(None, "tensor"),
            P(None, "tensor"),
            P("tensor", None),
            P(),
            P(None, "tensor"),
            P(None, "tensor"),
            P("tensor", None),
            P("dp", "ctx", None),
        ),
        out_specs=(
            P("dp", "ctx", None),
            P("dp", "ctx", None),
            P(("dp", "ctx")),
            P(("dp", "ctx"), "tensor"),
            P(("dp", "ctx"), "tensor"),
            P(("dp", "ctx"), "tensor"),
            P("tensor", ("dp", "ctx")),
            P(("dp", "ctx")),
            P(("dp", "ctx"), "tensor"),
            P(("dp", "ctx"), "tensor"),
            P("tensor", ("dp", "ctx")),
        ),
        check_vma=False,
    )
```

profile of v0, /device:TPU:0, one launch (start us, length us, event | category | flops | bytes accessed | tf_op | source)
XLA Modules:
  0.0 303.5 jit_solution(13862319216036640035)
XLA Ops:
  0.7 0.6 reshape_tile.3.frequency
  1.3 145.4 %shard_map.203 = (s32[1,1024]{1,0:T(1,128)}, f32[512,128]{1,0:T(8,128)}, f32[512,128]{1,0:T(8,128)}, bf16[512,512]{1,0:T(8,128)(2,1)}, bf16[1024,128]{1,0:T(8,12...) custom-call(bf16[512,2048]{1,0:T(8,128)(2,1)} %bitcast.12, ...), custom_call_target="tpu_custom_call" | custom-call | tf_op jit(solution)/shard_map/pallas_call | solution.py:646
  146.7 0.0 copy-start.3
  146.7 135.6 %shard_map.204 = (bf16[512,2048]{1,0:T(8,128)(2,1)}, bf16[512,2048]{1,0:T(8,128)(2,1)}, f32[8,256]{1,0:T(8,128)}, f32[256,640]{1,0:T(8,128)}, f32[256,512]{1,0:T...) custom-call(bf16[512,512]{1,0:T(8,128)(2,1)} %get-tuple-element.51.q, ...), custom_call_target="tpu_custom_call" | custom-call | tf_op jit(solution)/shard_map/pallas_call | solution.py:1082
  282.3 0.0 copy-done.3
  282.3 0.0 copy-start
  282.3 1.6 copy-done
  283.9 0.0 copy-start.1
  283.9 1.6 copy-done.1
  285.5 0.0 copy-start.2
  285.5 1.6 copy-done.2
  287.1 0.0 copy-start.4
  287.1 1.4 copy-done.4
  288.4 0.0 copy-start.5
  288.4 1.4 copy-done.5
  289.8 0.0 copy-start.6
  289.8 1.2 copy-done.6
  291.0 0.0 copy-start.7
  291.0 1.1 copy-done.7
  292.1 0.0 copy-start.8
  292.1 1.1 copy-done.8
  293.2 0.0 copy-start.9
  293.2 1.0 copy-done.9
  294.3 0.0 copy-start.10
  294.3 0.7 copy-done.10
  295.0 8.3 %shard_map.205 = (bf16[512,2048]{1,0:T(8,128)(2,1)}, bf16[512,2048]{1,0:T(8,128)(2,1)}, f32[1,256]{1,0:T(1,128)}, f32[256,512]{1,0:T(8,128)}, f32[64,256]{1,0:T(...) custom-call(bf16[512,2048]{1,0:T(8,128)(2,1)S(1)} %copy-done.1, ...), custom_call_target="tpu_custom_call" | custom-call | tf_op jit(solution)/shard_map/pallas_call | solution.py:1171
  (2 shorter events, 0.0 us)
Async XLA Ops:
  146.7 135.6 %copy-start.3 = (f32[256,1408]{1,0:T(8,128)S(1)}, f32[256,1408]{1,0:T(8,128)}, u32[]{:S(2)}) copy-start(f32[256,1408]{1,0:T(8,128)} %get-tuple-element.72.gate_any) | copy-start | bytes 4325380
  282.3 1.6 copy-start
  283.9 1.6 copy-start.1
  285.5 1.6 copy-start.2
  287.1 1.4 copy-start.4
  288.4 1.4 copy-start.5
  289.8 1.2 copy-start.6
  291.0 1.1 copy-start.7
  292.1 1.1 copy-start.8
  293.2 1.0 copy-start.9
  294.3 0.7 copy-start.10
where the time goes:
time: 304 us
  Pallas kernels  289 us (95%)
  local copies, waits for them, and re-layouts  13.3 us (4%)
    pallas_call x1, Pallas kernels, front_call(): pl.pallas_call(functools.partial(front_kernel, line_size, dp_size), out_s...  145 us
    pallas_call x1, Pallas kernels, back_call(): pl.pallas_call(functools.partial(back_kernel, line_size, dp_size), out_sh...  136 us
    unnamed x22, local copies, waits for them, and re-layouts  12.7 us
    pallas_call x1, Pallas kernels, settle_call(): pl.pallas_call(settle_kernel, out_shape=[jax.ShapeDtypeStruct(s, d) for s...  8.35 us

commit v1 on v0

--- a/solution.py
+++ b/solution.py
@@ -70,7 +70,8 @@
 
 
 class Line:
-    def __init__(self, line_size, own, finish, place, out_ref, held, acc_send, acc_recv, back_send, back_recv):
+    def __init__(self, line_size, own, finish, place, out_ref, held, acc_send, acc_recv, back_send, back_recv, base=0):
+        self.base = base
         self.last = line_size - 1
         self.here = lax.axis_index("tensor")
         self.own, self.finish, self.place = own, finish, place
@@ -84,15 +85,17 @@
         return self.last - self.here, self.here - 1, self.here + 1
 
     def acc_copy(self, stream, i, target):
-        ref = self.held.at[stream, i]
-        return remote(ref, ref, self.acc_sems[0].at[stream, i], self.acc_sems[1].at[stream, i], tensor=target)
+        at = i - self.base
+        ref = self.held.at[stream, at]
+        return remote(ref, ref, self.acc_sems[0].at[stream, at], self.acc_sems[1].at[stream, at], tensor=target)
 
     def rows_of(self, stream, i):
         return pl.ds(pl.multiple_of(self.place(stream, i), CHUNK), CHUNK)
 
     def back_copy(self, stream, i, target):
+        at = i - self.base
         ref = self.out_ref.at[self.rows_of(stream, i)]
-        return remote(ref, ref, self.back_sems[0].at[stream, i], self.back_sems[1].at[stream, i], tensor=target)
+        return remote(ref, ref, self.back_sems[0].at[stream, at], self.back_sems[1].at[stream, at], tensor=target)
 
     def step(self, k, begin=0, size=None):
         last, held = self.last, self.held
@@ -105,19 +108,20 @@
 
             @pl.when(inside & (place == 0))
             def _():
-                held[stream, i] = self.own(stream, i).astype(jnp.bfloat16)
+                held[stream, i - self.base] = self.own(stream, i).astype(jnp.bfloat16)
                 self.acc_copy(stream, i, after).start()
 
             @pl.when(inside & (place > 0) & (place < last))
             def _():
                 self.acc_copy(stream, i, after).wait_recv()
-                held[stream, i] = (held[stream, i].astype(jnp.float32) + self.own(stream, i)).astype(jnp.bfloat16)
+                at = i - self.base
+                held[stream, at] = (held[stream, at].astype(jnp.float32) + self.own(stream, i)).astype(jnp.bfloat16)
                 self.acc_copy(stream, i, after).start()
 
             @pl.when(inside & (place == last))
             def _():
                 self.acc_copy(stream, i, before).wait_recv()
-                total = held[stream, i].astype(jnp.float32) + self.own(stream, i)
+                total = held[stream, i - self.base].astype(jnp.float32) + self.own(stream, i)
                 self.out_ref[self.rows_of(stream, i)] = self.finish(stream, i, total).astype(jnp.bfloat16)
                 self.back_copy(stream, i, before).start()
 
@@ -133,7 +137,8 @@
                     self.back_copy(stream, j, before).start()
 
     def drain(self):
-        def sent(i, carry):
+        def sent(at, carry):
+            i = at + self.base
             for stream in (0, 1):
                 place, after, before = self.parts(stream)
 
@@ -150,8 +155,8 @@
         lax.fori_loop(0, self.count, sent, 0)
 
 
-def line_scratch(rows, width):
-    count = rows // 2 // CHUNK
+def line_scratch(rows, width, share=1):
+    count = rows // 2 // CHUNK // share
     return [
         pltpu.VMEM((2, count, CHUNK, width), jnp.bfloat16),
         *[pltpu.SemaphoreType.DMA((2, count))] * 4,
@@ -234,12 +239,12 @@
     n, dp_size,
     inputs_any, segments, frequency, gain_one, gain_two,
     query_weight_any, key_weight_any, value_weight_any, out_weight_any, gate_weight_any, up_weight_any, down_weight_any, upstream_any,
-    seg_out, cosine_out, sine_out, query_out, kv_out, log_out, mixed_out, normed_out, normed_two_out, up_out, inner_out, second_out,
-    attended_out, middle_out, grad_middle_out, land_gate, gain_out, own_gate,
+    seg_out, cosine_out, sine_out, query_out, kv_out, log_out, mixed_out, normed_cols, two_cols, upstream_cols, up_out, inner_out, second_out,
+    attended_out, middle_out, grad_middle_out, land_gate, land_up, own_gate, gain_out,
     seg_all, seg_row, seg_col, cosine, signed_sine,
-    inputs, normed, query_weight, kv_weight, out_weight, query, kv, kv_turned, logs, mixed, bias,
+    inputs, normed, kv_weight, query, kv, kv_turned, logs, mixed, bias,
     gate_weight, up_weight, down_weight, upstream, grad_inner, normed_two, gate, up, inner,
-    partial, middle, grad_middle, two_other, turned, send_gate,
+    partial, middle, grad_middle, two_other, turned, send_gate, send_up,
     load_sems, store_sems, core_send, core_recv, plane_send, plane_recv, *line_refs,
 ):
     span, width = inputs.shape
@@ -247,8 +252,8 @@
     row, core = lax.axis_index("dp"), lax.axis_index("ctx")
     half, block = span // 2, span // 4
     second, attended = normed, inputs
-    line_one, line_two = line_refs[:5], line_refs[5:]
-    count = line_one[0].shape[1]
+    line_one, line_two, line_three = line_refs[:5], line_refs[5:10], line_refs[10:]
+    count, heads = line_one[0].shape[1], query.shape[1]
     part = count // 2
 
     def load(at, src, dst):
@@ -263,6 +268,8 @@
         return (0, 2, 1, 3)[at] * block
 
     load_inputs = load(0, inputs_any, inputs)
+    query_weight = gate_weight.at[:, pl.ds(0, heads)]
+    out_weight = down_weight.at[pl.ds(0, heads)]
     load_query = load(1, query_weight_any, query_weight)
     load_kv = [
         load(2, key_weight_any, kv_weight.at[pl.ds(0, HEAD_DIM)]),
@@ -272,8 +279,6 @@
     load_up = [
         load(4 + b, upstream_any.at[pl.ds(b * block, block)], upstream.at[pl.ds(moved(b), block)]) for b in range(4)
     ]
-    load_down = load(8, down_weight_any, down_weight)
-    load_gate = load(9, gate_weight_any, gate_weight)
     load_up_weight = load(10, up_weight_any, up_weight)
     seg_all[core] = jnp.broadcast_to(segments[...], seg_all.shape[1:])
     greet(n, True, dp_size)
@@ -329,6 +334,7 @@
         for lanes in range(0, raw.shape[1], 128):
             rotated = rotate_lanes(raw[:, lanes : lanes + 128], cosine[rows], signed_sine[rows])
             query[rows, lanes : lanes + 128] = rotated.astype(jnp.bfloat16) * (HEAD_DIM ** -0.5)
+    load_gate = load(9, gate_weight_any, gate_weight)
 
     @pl.when(core == 1)
     def _():
@@ -383,6 +389,7 @@
         return carry
 
     lax.fori_loop(0, width // 512, out_tile, 0)
+    load_down = load(8, down_weight_any, down_weight)
 
     def rows_at(start):
         return pl.ds(pl.multiple_of(start, CHUNK), CHUNK)
@@ -411,6 +418,12 @@
 
     first = Line(n, own, finish_one, ordered, normed_two, *line_one)
     then = Line(n, own, finish_two, ordered, attended, *line_two)
+    third = Line(
+        n,
+        lambda stream, i: second[rows_at(ordered(stream, i))].astype(jnp.float32),
+        lambda stream, i, total: middle[kept_rows(i)] + total,
+        ordered, second, *line_three,
+    )
     tiles, rest = wide_tiles(hidden)
     tile_count = tiles + (1 if rest else 0)
 
@@ -456,8 +469,10 @@
     forward_steps, back_steps = -(-tile_count // each), width // 1024
     work = forward_steps + back_steps
     base_one = part + trip
-    base_two = max(count + trip, base_one + work + 1)
-    steps = base_two + work + part + trip
+    second_steps = width // 1024
+    base_two = max(count + trip, base_one + work + second_steps)
+    third_base = base_one + work + second_steps
+    steps = max(base_two + work + part + trip, third_base + part + trip)
 
     def store(at, src, dst):
         return pltpu.make_async_copy(src, dst, store_sems.at[at])
@@ -468,17 +483,51 @@
         ]
 
     early = [
-        store(0, query, query_out), store(1, kv, kv_out), store(2, logs, log_out), store(3, mixed, mixed_out),
+        store(0, query, query_out), store(1, kv, kv_out), store(2, logs, log_out), store(3, mixed, mixed_out.at[pl.ds(0, span)]),
         store(31, seg_row, seg_out), store(32, cosine, cosine_out),
         store(33, signed_sine, sine_out),
     ]
-    hidden_stores = [(5, normed_two, normed_two_out), (13, up, up_out), (17, inner, inner_out)]
+    own_slots, far_slots = [], []
+
+    def own_columns(src, dst):
+        made = []
+        for q in range(dp_size):
+            columns = pl.ds(pl.multiple_of((2 * q + core) * piece, piece), piece)
+            at = 34 + len(own_slots)
+            own_slots.append(at)
+            made.append(store(at, src.at[:, columns], dst.at[pl.ds(0, span), pl.ds(q * piece, piece)]))
+        return made
+
+    def far_copy(src, dst):
+        at = 3 + dp_size + len(far_slots)
+        far_slots.append(at)
+        return remote(src, dst, core_send.at[at], core_recv.at[at], ctx=1 - core)
+
+    def far_columns(src, dst):
+        made = []
+        for q in range(dp_size):
+            columns = pl.ds(pl.multiple_of((2 * q + 1 - core) * piece, piece), piece)
+            made.append(far_copy(src.at[:, columns], dst.at[pl.ds(span, span), pl.ds(q * piece, piece)]))
+        return made
+
+    normed_moves = [*own_columns(normed, normed_cols), *far_columns(normed, normed_cols)]
+    upstream_moves = [*own_columns(upstream, upstream_cols), *far_columns(upstream, upstream_cols)]
+    mixed_move = far_copy(mixed, mixed_out.at[pl.ds(span, span)])
+    hidden_moves = [
+        store(6, inner, inner_out.at[pl.ds(0, span)]), far_copy(inner, inner_out.at[pl.ds(span, span)]),
+        *own_columns(normed_two, two_cols),
+    ]
+    up_slot = 3 + dp_size + len(far_slots)
+    two_moves = [store(7, two_other, two_cols.at[pl.ds(span, span)]), store(5, up, up_out)]
+    second_stores = stores(21, second, second_out)
+    middle_store = store(29, middle, middle_out)
 
     def gate_swaps():
         made = [
             remote(
-                gate.at[pl.ds(0, span)], gate.at[pl.ds(span, span)], core_send.at[2], core_recv.at[2], ctx=1 - core
+                ref.at[pl.ds(0, span)], ref.at[pl.ds(span, span)], core_send.at[at], core_recv.at[at], ctx=1 - core
             )
+            for ref, at in ((gate, 2), (up, up_slot))
         ]
         for q in range(dp_size):
             columns = pl.ds(pl.multiple_of((2 * q + 1 - core) * piece, piece), piece)
@@ -493,49 +542,66 @@
     def peer_of(r):
         return lax.rem(row + 1 + r, dp_size)
 
-    def gate_copy(r):
-        return remote(send_gate.at[r], land_gate.at[r], plane_send.at[r], plane_recv.at[r], dp=peer_of(r))
-
-    def gate_piece(r):
+    sends, lands = (send_gate, send_up), (land_gate, land_up)
+
+    def gate_copy(w, r):
+        return remote(sends[w].at[r], lands[w].at[r], plane_send.at[w, r], plane_recv.at[w, r], dp=peer_of(r))
+
+    def turn_two(r):
         peer = peer_of(r)
         columns = pl.ds(pl.multiple_of((2 * peer + core) * piece, piece), piece)
         turned[:, 0:span] = normed_two[:, columns].T
         turned[:, span : 2 * span] = two_other[:, pl.ds(pl.multiple_of(peer * piece, piece), piece)].T
-        edges = [(low, min(low + 384, hidden)) for low in range(0, hidden, 384)]
-
-        @pl.when(r < dp_size - 1)
-        def _():
-            for low, high in edges:
-                send_gate[r, :, low:high] = jnp.dot(
-                    turned[...], gate[:, low:high], preferred_element_type=jnp.float32
-                ).astype(jnp.bfloat16)
-            gate_copy(r).start()
-
-        @pl.when(r == dp_size - 1)
-        def _():
-            for low, high in edges:
-                own_gate[:, low:high] = jnp.dot(turned[...], gate[:, low:high], preferred_element_type=jnp.float32)
-
-    keep_normed = store(4, normed, normed_out)
-    for made in [*early, keep_normed]:
+
+    edges = [(low, min(low + 384, hidden)) for low in range(0, hidden, 384)]
+
+    def gate_piece(w, r):
+        for low, high in edges:
+            sends[w][r, :, low:high] = jnp.dot(
+                turned[...], (gate, up)[w][:, low:high], preferred_element_type=jnp.float32
+            ).astype(jnp.bfloat16)
+        gate_copy(w, r).start()
+
+    def own_piece():
+        for low, high in edges:
+            partial[0:piece, low:high] = jnp.dot(turned[...], gate[:, low:high], preferred_element_type=jnp.float32)
+
+    own_store = store(4, partial.at[pl.ds(0, piece), pl.ds(0, hidden)], own_gate)
+
+    for made in [*early, *normed_moves, mixed_move]:
         made.start()
 
     def step(k, carry):
         first.step(k)
         then.step(k - (base_one + work), 0, part)
         then.step(k - (base_two + work), part, part)
+        third.step(k - third_base)
 
         @pl.when(k == 0)
         def _():
             for made in load_up:
                 made.wait()
+            for made in upstream_moves:
+                made.start()
+
+        @pl.when(k == 2)
+        def _():
             load_down.wait()
             load_gate.wait()
             load_up_weight.wait()
 
-        @pl.when((k >= 1) & (k <= tile_count))
-        def _():
-            each_tile(k - 1, inner_tile)
+        @pl.when((k >= 2) & (k < 2 + tile_count))
+        def _():
+            each_tile(k - 2, inner_tile)
+
+        @pl.when(k == base_one)
+        def _():
+            for made in normed_moves:
+                made.wait()
+
+        @pl.when(k == base_two)
+        def _():
+            middle_store.start()
 
         late = jnp.where(k >= base_two, 1, 0)
         phase = k - jnp.where(k >= base_two, base_two, base_one)
@@ -554,11 +620,15 @@
             for t in (0, 1):
                 back_tile(rows, 2 * (phase - forward_steps) + t)
 
+        @pl.when((phase >= work) & (phase < work + second_steps))
+        def _():
+            for t in (0, 1):
+                second_tile(rows, 2 * (phase - work) + t)
+
         @pl.when(k == base_two + work)
         def _():
-            for at, src, dst in hidden_stores:
-                for made in stores(at, src, dst):
-                    made.start()
+            for made in hidden_moves:
+                made.start()
 
         @pl.when(k == base_two + forward_steps)
         def _():
@@ -567,46 +637,57 @@
 
         @pl.when(k == base_two + work + 1)
         def _():
-            keep_normed.wait()
             for made in gate_swaps():
                 made.wait()
+            for made in two_moves:
+                made.start()
 
         gate_task = k - (base_two + work + 1)
 
-        @pl.when((gate_task >= 0) & (gate_task < dp_size))
-        def _():
-            gate_piece(gate_task)
-
-        after = gate_task - dp_size
-
-        @pl.when((after >= 0) & (after < 4))
-        def _():
-            for low in (0, half):
-                second_tile(pl.ds(low, half), after)
+        @pl.when((gate_task >= 0) & (gate_task < dp_size - 1))
+        def _():
+            turn_two(gate_task)
+            gate_piece(0, gate_task)
+
+            @pl.when(gate_task < dp_size - 2)
+            def _():
+                gate_piece(1, gate_task)
+
+        @pl.when(k == base_two + work + part + HOP * last)
+        def _():
+            turn_two(dp_size - 1)
+            own_piece()
+            own_store.start()
+
+        @pl.when(k == base_two + work + second_steps)
+        def _():
+            for b in (1, 3):
+                second_stores[b].start()
 
         return carry
 
     lax.fori_loop(0, steps, step, 0)
     late_stores = [
-        *stores(21, second, second_out), *stores(25, attended, attended_out),
-        store(29, middle, middle_out), store(30, grad_middle, grad_middle_out),
+        second_stores[0], second_stores[2], *stores(25, attended, attended_out), store(30, grad_middle, grad_middle_out),
     ]
     for made in late_stores:
         made.start()
     first.drain()
     then.drain()
+    third.drain()
 
     @pl.when(core == 0)
     def _():
         kv_copy().wait_send()
 
     for r in range(dp_size - 1):
-        gate_copy(r).wait()
-    for made in [*early, *late_stores]:
+        for w in ((0, 1) if r < dp_size - 2 else (0,)):
+            gate_copy(w, r).wait()
+    for made in [
+        *early, mixed_move, *upstream_moves, *hidden_moves, *two_moves, own_store, middle_store, second_stores[1], second_stores[3],
+        *late_stores,
+    ]:
         made.wait()
-    for at, src, dst in hidden_stores:
-        for made in stores(at, src, dst):
-            made.wait()
 
 
 def front_call(line_size, dp_size, operands):
@@ -620,34 +701,35 @@
     dma = pltpu.SemaphoreType.DMA
     outs = [
         ((1, 2 * span), jnp.int32), ((span, 128), full), ((span, 128), full),
-        ((span, heads), low), ((2 * span, 128), low), ((heads // HEAD_DIM, span), full), ((span, heads), low),
-        ((span, width), low), ((span, width), low), *[((span, hidden), low)] * 2, ((span, width), low),
+        ((span, heads), low), ((2 * span, 128), low), ((heads // HEAD_DIM, span), full), ((2 * span, heads), low),
+        *[((2 * span, width // 2), low)] * 3, *[((2 * span, hidden), low)] * 2, ((span, width), low),
         ((span, width), low), ((span // 2, width), full), ((span // 2, width), full),
-        ((dp_size - 1, piece, hidden), low), ((8, width), full), ((piece, hidden), full),
+        ((dp_size - 1, piece, hidden), low), ((dp_size - 2, piece, hidden), low), ((piece, hidden), full), ((8, width), full),
     ]
     scratch = [
         pltpu.VMEM((2, 8, span), jnp.int32), pltpu.VMEM((1, 2 * span), jnp.int32),
         pltpu.VMEM((2 * span, 1), jnp.int32), pltpu.VMEM((span, 128), full), pltpu.VMEM((span, 128), full),
-        pltpu.VMEM((span, width), low), pltpu.VMEM((span, width), low), pltpu.VMEM((width, heads), low),
-        pltpu.VMEM((128, width), low), pltpu.VMEM((heads, width), low), pltpu.VMEM((span, heads), low),
+        pltpu.VMEM((span, width), low), pltpu.VMEM((span, width), low),
+        pltpu.VMEM((128, width), low), pltpu.VMEM((span, heads), low),
         pltpu.VMEM((2 * span, 128), low), pltpu.VMEM((128, 2 * span), low),
         pltpu.VMEM((heads // HEAD_DIM, span), full), pltpu.VMEM((span, heads), low),
         pltpu.VMEM((2 * span, span // 2), full),
         pltpu.VMEM((width, hidden), low), pltpu.VMEM((width, hidden), low), pltpu.VMEM((hidden, width), low),
         pltpu.VMEM((span, width), low), pltpu.VMEM((span, hidden), full), pltpu.VMEM((span, width), low),
-        pltpu.VMEM((2 * span, hidden), low), *[pltpu.VMEM((span, hidden), low)] * 2,
+        *[pltpu.VMEM((2 * span, hidden), low)] * 2, pltpu.VMEM((span, hidden), low),
         pltpu.VMEM((span, width), full),
         pltpu.VMEM((span // 2, width), full), pltpu.VMEM((span // 2, width), full),
         pltpu.VMEM((span, width // 2), low), pltpu.VMEM((piece, 2 * span), low),
-        pltpu.VMEM((dp_size - 1, piece, hidden), low),
-        dma((12,)), dma((34,)), dma((3 + dp_size,)), dma((3 + dp_size,)), dma((dp_size - 1,)), dma((dp_size - 1,)),
-        *line_scratch(span, width), *line_scratch(span, width),
+        pltpu.VMEM((dp_size - 1, piece, hidden), low), pltpu.VMEM((dp_size - 2, piece, hidden), low),
+        dma((12,)), dma((34 + 3 * dp_size,)), dma((6 + 3 * dp_size,)), dma((6 + 3 * dp_size,)),
+        dma((2, dp_size - 1)), dma((2, dp_size - 1)),
+        *line_scratch(span, width), *line_scratch(span, width), *line_scratch(span, width, 2),
     ]
     return pl.pallas_call(
         functools.partial(front_kernel, line_size, dp_size),
         out_shape=[jax.ShapeDtypeStruct(s, d) for s, d in outs],
         in_specs=[outside] + [vmem] * 4 + [outside] * 8,
-        out_specs=[outside] * 16 + [vmem] * 2,
+        out_specs=[outside] * 19 + [vmem],
         scratch_shapes=scratch,
         compiler_params=pltpu.CompilerParams(
             collective_id=1, has_side_effects=True, vmem_limit_bytes=FRONT_MIB * MIB
@@ -657,12 +739,12 @@
 
 def back_kernel(
     n, dp_size,
-    query_any, kv_any, logs, mixed_any, cosine, signed_sine, seg_row, inputs_any, normed_any, normed_two_any,
+    query_any, kv_any, logs, mixed_any, cosine, signed_sine, seg_row, inputs_any, normed_any, two_any, upstream_any,
     up_any, inner_any, second_any, attended_any, middle_any, grad_middle_any, gain_one, gain_two_grad,
-    query_weight_any, key_weight_any, value_weight_any, out_weight_any, upstream_any,
+    query_weight_any, key_weight_any, value_weight_any, out_weight_any,
     layer_out, grad_inputs, grad_gains, grad_qkv, own_out, grad_up, own_down,
     land_up, land_down, land_qkv, land_out,
-    query, kv, kv_turned, grad_mixed, mixed, attended, normed_cols, attended_cols, two_cols, upstream_cols,
+    query, kv, kv_turned, grad_mixed, mixed, attended, normed_cols, two_cols, upstream_cols, attended_other,
     up, inner, pre, query_weight, kv_weight, out_weight, grad_middle, middle, inputs,
     ring, send_qkv, send_out, turned, seg_col, bias, kv_grad, kv_grad_other,
     gain_line, gain_land, gain_sum, gain_plane,
@@ -674,7 +756,7 @@
     here, row, core = lax.axis_index("tensor"), lax.axis_index("dp"), lax.axis_index("ctx")
     half = span // 2
     line_out, line_in = line_refs[:5], line_refs[5:]
-    count = line_out[0].shape[1]
+    count, part = line_in[0].shape[1], line_out[0].shape[1]
     last = n - 1
     loads = []
 
@@ -685,55 +767,32 @@
         return made
 
     own_half = pl.ds(pl.multiple_of(jnp.where(here == 0, half, 0), half), half)
-    first_loads = [
-        load(second_any, layer_out), load(middle_any, middle),
-        load(attended_any, attended), load(out_weight_any, out_weight), load(query_any, query), load(kv_any, kv),
-    ]
-
-    def load_cols(src, dst):
-        made = []
-        for q in range(dp_size):
-            block = pl.multiple_of((2 * q + core) * piece, piece)
-            made.append(load(src.at[:, pl.ds(block, piece)], dst.at[pl.ds(0, span), pl.ds(q * piece, piece)]))
-        return made
-
-    up_loads = [load(up_any, up.at[pl.ds(0, span)]), *load_cols(normed_two_any, two_cols)]
-    inner_loads = [load(inner_any, inner.at[pl.ds(0, span)]), *load_cols(upstream_any, upstream_cols)]
+    line_loads = [load(second_any, layer_out), load(middle_any, middle)]
+    mixed_loads = [load(attended_any, attended), load(out_weight_any, out_weight)]
+    attend_loads = [load(query_any, query), load(kv_any, kv)]
+
+    up_loads = [load(two_any, two_cols), load(up_any, up)]
+    inner_loads = [load(upstream_any, upstream_cols), load(inner_any, inner)]
     late_loads = [
         load(query_weight_any, query_weight), load(key_weight_any, kv_weight.at[pl.ds(0, HEAD_DIM)]),
         load(value_weight_any, kv_weight.at[pl.ds(HEAD_DIM, HEAD_DIM)]),
         load(grad_middle_any, grad_middle), load(inputs_any.at[own_half], inputs),
-        load(mixed_any, mixed.at[pl.ds(0, span)]), *load_cols(normed_any, normed_cols),
-        *load_cols(attended_any, attended_cols),
+        load(mixed_any, mixed), load(normed_any, normed_cols),
     ]
     greet(n, True, dp_size, full_line=True)
-    slots = []
-
-    def swap(src, dst):
-        at = len(slots)
-        slots.append(at)
-        return remote(src, dst, core_send.at[at], core_recv.at[at], ctx=1 - core)
-
-    def swap_rows(src, dst):
-        return swap(src, dst.at[pl.ds(span, span)])
-
-    def swap_cols(src, dst):
+    pre_slot, kv_slot = dp_size, dp_size + 1
+
+    def attended_swaps():
         made = []
         for q in range(dp_size):
-            block = pl.multiple_of((2 * q + 1 - core) * piece, piece)
+            columns = pl.ds(pl.multiple_of((2 * q + 1 - core) * piece, piece), piece)
             made.append(
-                swap(src.at[:, pl.ds(block, piece)], dst.at[pl.ds(span, span), pl.ds(q * piece, piece)])
+                remote(
+                    attended.at[:, columns], attended_other.at[:, pl.ds(q * piece, piece)],
+                    core_send.at[q], core_recv.at[q], ctx=1 - core,
+                )
             )
         return made
-
-    up_swaps = [swap_rows(up_any, up), *swap_cols(normed_two_any, two_cols)]
-    inner_swaps = [swap_rows(inner_any, inner), *swap_cols(upstream_any, upstream_cols)]
-    late_swaps = [
-        swap_rows(mixed_any, mixed), *swap_cols(attended_any, attended_cols), *swap_cols(normed_any, normed_cols),
-    ]
-    for made in [*up_swaps, *inner_swaps, *late_swaps]:
-        made.start()
-    pre_slot, kv_slot = len(slots), len(slots) + 1
 
     def pre_swap():
         return remote(
@@ -750,9 +809,8 @@
     gain_line[1:2, :] = gain_two_grad[0:1, :]
     kv_grad[...] = jnp.zeros_like(kv_grad)
     seg_col[...] = jnp.broadcast_to(seg_row[...], (8, 2 * span)).T[:, 0:1]
-    for made in first_loads:
+    for made in line_loads:
         made.wait()
-    kv_turned[...] = kv[...].T
 
     def rows_at(start):
         return pl.ds(pl.multiple_of(start, CHUNK), CHUNK)
@@ -774,7 +832,8 @@
         )
 
     out_line = Line(
-        n, lambda s, i: layer_out[rows_at(plain(s, i))].astype(jnp.float32), finish_out, plain, layer_out, *line_out
+        n, lambda s, i: layer_out[rows_at(plain(s, i))].astype(jnp.float32), finish_out, plain, layer_out, *line_out,
+        base=count - part,
     )
     in_line = Line(
         n, lambda s, i: grad_inputs[rows_at(plain(s, i))].astype(jnp.float32), finish_in, plain, grad_inputs, *line_in
@@ -855,6 +914,12 @@
         block = pl.multiple_of(peer_of(r) * piece, piece)
         turned[...] = cols[:, pl.ds(block, piece)].T
 
+    def turn_attended(r):
+        peer = peer_of(r)
+        columns = pl.ds(pl.multiple_of((2 * peer + core) * piece, piece), piece)
+        turned[:, 0:span] = attended[:, columns].T
+        turned[:, span : 2 * span] = attended_other[:, pl.ds(pl.multiple_of(peer * piece, piece), piece)].T
+
     def tiles_of(stacked):
         wide = stacked.shape[1]
         return [(low, min(low + 384, wide)) for low in range(0, wide, 384)]
@@ -862,29 +927,23 @@
     def piece_value(stacked, low, high):
         return jnp.dot(turned[...], stacked[:, low:high], preferred_element_type=jnp.float32)
 
-    landings = (land_up, land_down)
     others = dp_size - 1
 
-    def ring_copy(w, r, at):
-        return remote(
-            ring.at[at], landings[w].at[r], ring_send.at[at], ring_recv.at[w, r], dp=peer_of(r)
-        )
-
-    def ring_piece(w, r, stacked, own):
-        at = others * w + r
-
-        @pl.when(r < dp_size - 1)
-        def _():
-            slot = at
-
-            for low, high in tiles_of(stacked):
-                ring[slot, :, low:high] = piece_value(stacked, low, high).astype(jnp.bfloat16)
-            ring_copy(w, r, at).start()
-
-        @pl.when(r == dp_size - 1)
-        def _():
-            for low, high in tiles_of(stacked):
-                own[:, low:high] = piece_value(stacked, low, high)
+    def ring_copy(at):
+        r = others - 1 if at == 0 else at - 1
+        land = land_up.at[0] if at == 0 else land_down.at[at - 1]
+        return remote(ring.at[at], land, ring_send.at[at], ring_recv.at[at], dp=peer_of(r))
+
+    def ring_piece(at, cols, stacked):
+        turn(others - 1 if at == 0 else at - 1, cols)
+        for low, high in tiles_of(stacked):
+            ring[at, :, low:high] = piece_value(stacked, low, high).astype(jnp.bfloat16)
+        ring_copy(at).start()
+
+    def kept_piece(cols, stacked, own):
+        turn(others, cols)
+        for low, high in tiles_of(stacked):
+            own[:, low:high] = piece_value(stacked, low, high)
 
     sends, lands = (send_qkv, send_out), (land_qkv, land_out)
 
@@ -913,101 +972,7 @@
             for hop in hops
         ]
 
-    lag = tasks + 2
-    ffn_tasks = 2 * dp_size
-    out_base = max(ffn_tasks + 1, lag + 1)
-    steps = max(lag + count + 2 * HOP * last, out_base + dp_size)
-
-    def step(k, carry):
-        out_line.step(k)
-        in_line.step(k - lag)
-
-        @pl.when(k == 0)
-        def _():
-            grad_mixed[...] = turned_dot(attended[...], out_weight[...]).astype(jnp.bfloat16)
-
-        @pl.when((k >= 1) & (k <= tasks))
-        def _():
-            attend_task(k - 1)
-
-        @pl.when((k == tasks) & (core == 1))
-        def _():
-            kv_swap().start()
-
-        @pl.when(k == 1)
-        def _():
-            for made in [*up_loads, *up_swaps]:
-                made.wait()
-
-        @pl.when(k == dp_size + 1)
-        def _():
-            for made in [*inner_loads, *inner_swaps]:
-                made.wait()
-
-        @pl.when(k == tasks)
-        def _():
-            for made in late_loads:
-                made.wait()
-            for made in late_swaps:
-                made.wait()
-
-        @pl.when(k == tasks + 1)
-        def _():
-            finish_pre()
-            in_products()
-            pre_swap().start()
-
-        r = k - 1
-
-        @pl.when((r >= 0) & (r < dp_size))
-        def _():
-            turn(r, two_cols)
-            ring_piece(0, r, up, grad_up)
-
-        @pl.when((r >= dp_size) & (r < 2 * dp_size))
-        def _():
-            turn(r - dp_size, upstream_cols)
-            ring_piece(1, r - dp_size, inner, own_down)
-
-        @pl.when(k == out_base)
-        def _():
-            pre_swap().wait()
-
-        at = k - out_base
-
-        @pl.when((at >= 0) & (at < dp_size))
-        def _():
-            turn(at, attended_cols)
-            plane_piece(1, at, mixed, own_out)
-            turn(at, normed_cols)
-            plane_piece(0, at, pre, grad_qkv)
-
-        @pl.when(k == lag + count + HOP * last - 1)
-        def _():
-            for owner in (0, last):
-
-                @pl.when(here == owner)
-                def _():
-                    for made in line_copies(owner, range(1, n)):
-                        made.start()
-
-        return carry
-
-    lax.fori_loop(0, steps, step, 0)
     shard = width // (2 * dp_size)
-    gain_sum[...] = jnp.zeros_like(gain_sum)
-    for owner in (0, last):
-        slot = 0 if owner == 0 else 1
-
-        @pl.when(here == owner)
-        def _():
-            gain_sum[...] += gain_line[...]
-
-        @pl.when(here != owner)
-        def _():
-            line_copies(owner, (1,))[0].wait_recv()
-            gain_sum[...] += gain_land[slot]
-
     shards = 2 * dp_size
     place = 2 * row + core
 
@@ -1019,8 +984,112 @@
             dp=peer // 2, ctx=lax.rem(peer, 2),
         )
 
-    for r in range(shards - 1):
-        spread(r).start()
+    def gather_gains():
+        gain_sum[...] = jnp.zeros_like(gain_sum)
+        for owner in (0, last):
+            slot = 0 if owner == 0 else 1
+
+            @pl.when(here == owner)
+            def _():
+                gain_sum[...] += gain_line[...]
+
+            @pl.when(here != owner)
+            def _():
+                line_copies(owner, (1,))[0].wait_recv()
+                gain_sum[...] += gain_land[slot]
+        for r in range(shards - 1):
+            spread(r).start()
+
+    lag = tasks + 2
+    ring_steps = [1, 3, 6] + [lag + at for at in range(dp_size - 3)]
+    out_base = lag + 1
+    steps = max(lag + count + 2 * HOP * last, out_base + dp_size)
+
+    def step(k, carry):
+        out_line.step(k, count - part, part)
+        in_line.step(k - lag)
+
+        @pl.when(k == 0)
+        def _():
+            for made in [*mixed_loads, *attend_loads]:
+                made.wait()
+            for made in attended_swaps():
+                made.start()
+            kv_turned[...] = kv[...].T
+            grad_mixed[...] = turned_dot(attended[...], out_weight[...]).astype(jnp.bfloat16)
+
+        @pl.when((k >= 1) & (k <= tasks))
+        def _():
+            attend_task(k - 1)
+
+        @pl.when((k == tasks) & (core == 1))
+        def _():
+            kv_swap().start()
+
+        @pl.when(k == 1)
+        def _():
+            for made in up_loads:
+                made.wait()
+
+        @pl.when(k == ring_steps[1])
+        def _():
+            for made in inner_loads:
+                made.wait()
+
+        @pl.when(k == tasks)
+        def _():
+            for made in [*late_loads, *attended_swaps()]:
+                made.wait()
+
+        @pl.when(k == tasks + 1)
+        def _():
+            finish_pre()
+            in_products()
+            pre_swap().start()
+
+        for at in range(dp_size):
+
+            @pl.when(k == ring_steps[at])
+            def _():
+                ring_piece(at, *((two_cols, up) if at == 0 else (upstream_cols, inner)))
+
+        @pl.when(k == lag + dp_size)
+        def _():
+            kept_piece(two_cols, up, grad_up)
+
+        @pl.when(k == lag + dp_size + 1)
+        def _():
+            kept_piece(upstream_cols, inner, own_down)
+
+        @pl.when(k == out_base)
+        def _():
+            pre_swap().wait()
+
+        at = k - out_base
+
+        @pl.when((at >= 0) & (at < dp_size))
+        def _():
+            turn_attended(at)
+            plane_piece(1, at, mixed, own_out)
+            turn(at, normed_cols)
+            plane_piece(0, at, pre, grad_qkv)
+
+        @pl.when(k == lag + count + HOP * last - 1)
+        def _():
+            for owner in (0, last):
+
+                @pl.when(here == owner)
+                def _():
+                    for made in line_copies(owner, range(1, n)):
+                        made.start()
+
+        @pl.when(k == lag + count + HOP * last + 3)
+        def _():
+            gather_gains()
+
+        return carry
+
+    lax.fori_loop(0, steps, step, 0)
     out_line.drain()
     in_line.drain()
 
@@ -1028,9 +1097,10 @@
     def _():
         kv_swap().wait_send()
 
+    for at in range(dp_size):
+        ring_copy(at).wait()
     for r in range(others):
         for w in (0, 1):
-            ring_copy(w, r, others * w + r).wait()
             plane_copy(w, r).wait()
     grad_gains[...] = gain_sum[:, pl.ds(pl.multiple_of(place * shard, shard), shard)]
     for r in range(shards - 1):
@@ -1045,9 +1115,9 @@
 
 
 def back_call(line_size, dp_size, operands):
-    query, kv, logs, mixed = operands[:4]
+    query = operands[0]
     span, heads = query.shape
-    width, hidden = operands[8].shape[1], operands[10].shape[1]
+    width, hidden = operands[7].shape[1], operands[11].shape[1]
     piece = width // (2 * dp_size)
     wide = heads + 128
     low, full = jnp.bfloat16, jnp.float32
@@ -1057,28 +1127,28 @@
     outs = [
         ((span, width), low), ((span, width), low), ((8, piece), full), ((piece, wide), full), ((piece, heads), full),
         ((piece, hidden), full), ((piece, hidden), full),
-        *[((others, piece, hidden), low)] * 2, ((others, piece, wide), low), ((others, piece, heads), low),
+        ((1, piece, hidden), low), ((others, piece, hidden), low), ((others, piece, wide), low), ((others, piece, heads), low),
     ]
-    core_copies = 3 + 4 * dp_size + 2
+    core_copies = dp_size + 2
     scratch = [
         pltpu.VMEM((span, heads), low), pltpu.VMEM((2 * span, 128), low), pltpu.VMEM((128, 2 * span), low),
         pltpu.VMEM((span, heads), low), pltpu.VMEM((2 * span, heads), low), pltpu.VMEM((span, width), low),
-        *[pltpu.VMEM((2 * span, width // 2), low)] * 4,
+        *[pltpu.VMEM((2 * span, width // 2), low)] * 3, pltpu.VMEM((span, width // 2), low),
         *[pltpu.VMEM((2 * span, hidden), low)] * 2, pltpu.VMEM((2 * span, wide), low),
         pltpu.VMEM((width, heads), low), pltpu.VMEM((128, width), low), pltpu.VMEM((heads, width), low),
         pltpu.VMEM((span // 2, width), full), pltpu.VMEM((span // 2, width), full), pltpu.VMEM((span // 2, width), low),
-        pltpu.VMEM((2 * others, piece, hidden), low), pltpu.VMEM((others, piece, wide), low),
+        pltpu.VMEM((dp_size, piece, hidden), low), pltpu.VMEM((others, piece, wide), low),
         pltpu.VMEM((others, piece, heads), low),
         pltpu.VMEM((piece, 2 * span), low), pltpu.VMEM((2 * span, 1), jnp.int32), pltpu.VMEM((2 * span, span // 2), full),
         pltpu.VMEM((2 * span, 128), full), pltpu.VMEM((span, 128), full),
         pltpu.VMEM((8, width), full), pltpu.VMEM((2, 8, width), full), pltpu.VMEM((8, width), full),
         pltpu.VMEM((2 * dp_size - 1, 8, piece), full),
-        dma((17 + 4 * dp_size + 6,)), dma((core_copies,)), dma((core_copies,)),
-        dma((2 * others,)), dma((2, others)), dma((2, others)), dma((2, others)),
+        dma((17,)), dma((core_copies,)), dma((core_copies,)),
+        dma((dp_size,)), dma((dp_size,)), dma((2, others)), dma((2, others)),
         dma((2, line_size - 1)), dma((2,)), dma((2 * dp_size - 1,)), dma((2 * dp_size - 1,)),
-        *line_scratch(span, width), *line_scratch(span, width),
+        *line_scratch(span, width, 2), *line_scratch(span, width),
     ]
-    spaces = [outside, outside, vmem, outside, vmem, vmem, vmem] + [outside] * 9 + [vmem, vmem] + [outside] * 5
+    spaces = [outside, outside, vmem, outside, vmem, vmem, vmem] + [outside] * 10 + [vmem, vmem] + [outside] * 4
     return pl.pallas_call(
         functools.partial(back_kernel, line_size, dp_size),
         out_shape=[jax.ShapeDtypeStruct(s, d) for s, d in outs],
@@ -1093,17 +1163,22 @@
 
 def settle_kernel(
     layer_any, inputs_any, gains, qkv_any, out_any, gate_any, up_any, down_any,
-    land_gate, land_up, land_down, land_qkv, land_out,
+    land_gate, land_up, land_up_last, land_down, land_qkv, land_out,
     layer_out, grad_inputs, gain_one, grad_query, grad_key, grad_value, grad_out, gain_two, grad_gate, grad_up, grad_down,
     own_qkv, own_out, own_gate, own_up, own_down, far_qkv, far_out, far_gate, far_up, far_down,
-    turned_kv, turned_out, turned_down, in_sems, out_sems,
+    turned_kv, turned_out, turned_down, layer_held, inputs_held, in_sems, out_sems,
 ):
-    whole = [
-        pltpu.make_async_copy(layer_any, layer_out, out_sems.at[0]),
-        pltpu.make_async_copy(inputs_any, grad_inputs, out_sems.at[1]),
+    whole, early = [], land_up.shape[0]
+    passed = [
+        pltpu.make_async_copy(layer_any, layer_held, in_sems.at[0, 5]),
+        pltpu.make_async_copy(inputs_any, inputs_held, in_sems.at[1, 5]),
+        pltpu.make_async_copy(land_up_last, far_up.at[pl.ds(early, 1)], in_sems.at[0, 6]),
     ]
     owns = ((qkv_any, own_qkv), (out_any, own_out), (gate_any, own_gate), (up_any, own_up), (down_any, own_down))
-    fars = ((land_qkv, far_qkv), (land_out, far_out), (land_gate, far_gate), (land_up, far_up), (land_down, far_down))
+    fars = (
+        (land_qkv, far_qkv), (land_out, far_out), (land_gate, far_gate), (land_up, far_up.at[pl.ds(0, early)]),
+        (land_down, far_down),
+    )
     loads = [
         (
             pltpu.make_async_copy(*own, in_sems.at[0, at]),
@@ -1114,7 +1189,7 @@
     for pair in loads:
         for made in pair:
             made.start()
-    for made in whole:
+    for made in passed:
         made.start()
     gain_one[...] = gains[0:1]
     gain_two[...] = gains[1:2]
@@ -1140,10 +1215,15 @@
     put(4, turned_kv.at[pl.ds(HEAD_DIM, HEAD_DIM)], grad_value)
     turned_out[...] = settle(1, own_out, far_out).T
     put(5, turned_out, grad_out)
+    passed[0].wait()
+    put(0, layer_held, layer_out)
     own_gate[...] = settle(2, own_gate, far_gate)
     put(6, own_gate, grad_gate)
+    passed[2].wait()
     own_up[...] = settle(3, own_up, far_up)
     put(7, own_up, grad_up)
+    passed[1].wait()
+    put(1, inputs_held, grad_inputs)
     turned_down[...] = settle(4, own_down, far_down).T
     put(8, turned_down, grad_down)
     for made in whole:
@@ -1166,15 +1246,16 @@
     scratch = [
         *[pltpu.VMEM(shape, full) for shape in shapes], *[pltpu.VMEM((others, *shape), low) for shape in shapes],
         pltpu.VMEM((wide - heads, piece), full), pltpu.VMEM((heads, piece), full), pltpu.VMEM((hidden, piece), full),
-        pltpu.SemaphoreType.DMA((2, 5)), pltpu.SemaphoreType.DMA((9,)),
+        pltpu.VMEM(layer_out.shape, low), pltpu.VMEM(layer_out.shape, low),
+        pltpu.SemaphoreType.DMA((2, 7)), pltpu.SemaphoreType.DMA((9,)),
     ]
     return pl.pallas_call(
         settle_kernel,
         out_shape=[jax.ShapeDtypeStruct(s, d) for s, d in outs],
-        in_specs=[outside, outside, vmem] + [outside] * 10,
+        in_specs=[outside, outside, vmem] + [outside] * 11,
         out_specs=[outside, outside, vmem] + [outside] * 4 + [vmem] + [outside] * 3,
         scratch_shapes=scratch,
-        compiler_params=pltpu.CompilerParams(vmem_limit_bytes=40 * MIB),
+        compiler_params=pltpu.CompilerParams(vmem_limit_bytes=62 * MIB),
     )(*operands)
 
 
@@ -1420,8 +1501,8 @@
     gain_one, gain_two = attention_gain.reshape(1, -1), feedforward_gain.reshape(1, -1)
     key_turned, value_turned = key_weight.T, value_weight.T
     (
-        seg_row, cosine, signed_sine, query, kv, logs, mixed, normed, normed_two, up, inner, second, attended,
-        middle, grad_middle, land_gate, gain_grad, own_gate,
+        seg_row, cosine, signed_sine, query, kv, logs, mixed, normed, two, upstream_cols, up, inner, second, attended,
+        middle, grad_middle, land_gate, land_up, own_gate, gain_grad,
     ) = front_call(
         line_size, dp_size,
         (
@@ -1430,19 +1511,20 @@
         ),
     )
     (
-        layer_out, grad_inputs, gains, own_qkv, own_out, own_up, own_down, land_up, land_down, land_qkv, land_out
+        layer_out, grad_inputs, gains, own_qkv, own_out, own_up, own_down, land_up_last, land_down, land_qkv,
+        land_out,
     ) = back_call(
         line_size, dp_size,
         (
-            query, kv, logs, mixed, cosine, signed_sine, seg_row, flat_inputs, normed, normed_two,
+            query, kv, logs, mixed, cosine, signed_sine, seg_row, flat_inputs, normed, two, upstream_cols,
             up, inner, second, attended, middle, grad_middle, gain_one, gain_grad,
-            query_weight, key_turned, value_turned, out_weight, upstream,
+            query_weight, key_turned, value_turned, out_weight,
         ),
     )
     layer_out, grad_inputs, gain_a, grad_query, grad_key, grad_value, grad_out, gain_b, *ffn = settle_call(
         (
             layer_out, grad_inputs, gains, own_qkv, own_out, own_gate, own_up, own_down,
-            land_gate, land_up, land_down, land_qkv, land_out,
+            land_gate, land_up, land_up_last, land_down, land_qkv, land_out,
         )
     )
     shape = (1, span_len, model_width)
@@ -1457,7 +1539,7 @@
     span_len, model_width = inputs.shape[1:]
     dp_size, ctx_size, line_size = mesh.shape["dp"], mesh.shape["ctx"], mesh.shape["tensor"]
     piece = model_width // (dp_size * ctx_size)
-    fits = inputs.shape[0] == 1 and ctx_size == 2 and dp_size > 1 and line_size > 1
+    fits = inputs.shape[0] == 1 and ctx_size == 2 and dp_size > 2 and line_size > 1
     if fits and piece % 128 == 0 and span_len % (2 * CHUNK) == 0:
         return fast_body(*arrays)
     return plain_body(*arrays)

time: 304 us -> 301 us (level)
  local copies, waits for them, and re-layouts: 13.3 us -> 0.6 us
  Pallas kernels: 289 us -> 300 us
    pallas_call x1, Pallas kernels: 145 us -> 172 us  [front_call(): pl.pallas_call(functools.partial(front_kernel, line_size, dp_size), out_s...]
    pallas_call x1, Pallas kernels: 136 us -> 117 us  [back_call(): pl.pallas_call(functools.partial(back_kernel, line_size, dp_size), out_sh...]
    unnamed x22 -> x0, local copies, waits for them, and re-layouts: 12.7 us -> none
where the time goes in v1:
time: 301 us
  Pallas kernels  300 us (100%)
    pallas_call x1, Pallas kernels, front_call(): pl.pallas_call(functools.partial(front_kernel, line_size, dp_size), out_s...  172 us
    pallas_call x1, Pallas kernels, back_call(): pl.pallas_call(functools.partial(back_kernel, line_size, dp_size), out_sh...  117 us
    pallas_call x1, Pallas kernels, settle_call(): pl.pallas_call(settle_kernel, out_shape=[jax.ShapeDtypeStruct(s, d) for s...  10.7 us

profile of v1, /device:TPU:0, one launch (start us, length us, event | category | flops | bytes accessed | tf_op | source)
XLA Modules:
  0.0 301.2 jit_solution(9939815790127513675)
XLA Ops:
  0.7 0.6 reshape_tile.3.frequency
  1.3 171.9 %shard_map.203 = (s32[1,1024]{1,0:T(1,128)}, f32[512,128]{1,0:T(8,128)}, f32[512,128]{1,0:T(8,128)}, bf16[512,512]{1,0:T(8,128)(2,1)}, bf16[1024,128]{1,0:T(8,12...) custom-call(bf16[512,2048]{1,0:T(8,128)(2,1)} %bitcast.12, ...), custom_call_target="tpu_custom_call" | custom-call | tf_op jit(solution)/shard_map/pallas_call | solution.py:728
  173.2 117.1 %shard_map.204 = (bf16[512,2048]{1,0:T(8,128)(2,1)}, bf16[512,2048]{1,0:T(8,128)(2,1)}, f32[8,256]{1,0:T(8,128)}, f32[256,640]{1,0:T(8,128)}, f32[256,512]{1,0:T...) custom-call(bf16[512,512]{1,0:T(8,128)(2,1)} %get-tuple-element.53.q, ...), custom_call_target="tpu_custom_call" | custom-call | tf_op jit(solution)/shard_map/pallas_call | solution.py:1152
  290.3 10.7 %shard_map.205 = (bf16[512,2048]{1,0:T(8,128)(2,1)}, bf16[512,2048]{1,0:T(8,128)(2,1)}, f32[1,256]{1,0:T(1,128)}, f32[256,512]{1,0:T(8,128)}, f32[64,256]{1,0:T(...) custom-call(bf16[512,2048]{1,0:T(8,128)(2,1)} %get-tuple-element.70., ...), custom_call_target="tpu_custom_call" | custom-call | tf_op jit(solution)/shard_map/pallas_call | solution.py:1252
  (2 shorter events, 0.0 us)

commit v2 on v1

--- a/solution.py
+++ b/solution.py
@@ -26,8 +26,10 @@
 
 
 MESH = pl.DeviceIdType.MESH
-CHUNK = 16
-HOP = 2
+CHUNK, HOP = 16, 2
+BACK_CHUNK, BACK_HOP = 32, 2
+TASKS = 1
+RINGS = [1, 2, 4]
 MIB = 1 << 20
 FRONT_MIB, BACK_MIB = 62, 62
 
@@ -70,14 +72,14 @@
 
 
 class Line:
-    def __init__(self, line_size, own, finish, place, out_ref, held, acc_send, acc_recv, back_send, back_recv, base=0):
-        self.base = base
+    def __init__(self, line_size, own, finish, place, out_ref, held, acc_send, acc_recv, back_send, back_recv, base=0, hop=HOP):
+        self.base, self.hop = base, hop
         self.last = line_size - 1
         self.here = lax.axis_index("tensor")
         self.own, self.finish, self.place = own, finish, place
         self.out_ref, self.held = out_ref, held
         self.acc_sems, self.back_sems = (acc_send, acc_recv), (back_send, back_recv)
-        self.count = held.shape[1]
+        self.count, self.chunk = held.shape[1:3]
 
     def parts(self, stream):
         if stream == 0:
@@ -90,7 +92,7 @@
         return remote(ref, ref, self.acc_sems[0].at[stream, at], self.acc_sems[1].at[stream, at], tensor=target)
 
     def rows_of(self, stream, i):
-        return pl.ds(pl.multiple_of(self.place(stream, i), CHUNK), CHUNK)
+        return pl.ds(pl.multiple_of(self.place(stream, i), self.chunk), self.chunk)
 
     def back_copy(self, stream, i, target):
         at = i - self.base
@@ -98,43 +100,52 @@
         return remote(ref, ref, self.back_sems[0].at[stream, at], self.back_sems[1].at[stream, at], tensor=target)
 
     def step(self, k, begin=0, size=None):
+        size = self.count if size is None else size
+
+        @pl.when((k >= 0) & (k < size + 2 * self.hop * self.last))
+        def _():
+            for stream in (0, 1):
+                self.stream_step(k, stream, begin, size)
+
+    def stream_step(self, k, stream, begin, size):
         last, held = self.last, self.held
-        size = self.count if size is None else size
-        for stream in (0, 1):
-            place, after, before = self.parts(stream)
-            due = k - HOP * place
-            inside = (due >= 0) & (due < size)
-            i = begin + due
-
-            @pl.when(inside & (place == 0))
+        place, after, before = self.parts(stream)
+        due = k - self.hop * place
+        i = begin + due
+        at = i - self.base
+
+        @pl.when((due >= 0) & (due < size))
+        def _():
+            @pl.when(place == 0)
             def _():
-                held[stream, i - self.base] = self.own(stream, i).astype(jnp.bfloat16)
+                held[stream, at] = self.own(stream, i).astype(jnp.bfloat16)
                 self.acc_copy(stream, i, after).start()
 
-            @pl.when(inside & (place > 0) & (place < last))
+            @pl.when(place > 0)
             def _():
                 self.acc_copy(stream, i, after).wait_recv()
-                at = i - self.base
-                held[stream, at] = (held[stream, at].astype(jnp.float32) + self.own(stream, i)).astype(jnp.bfloat16)
-                self.acc_copy(stream, i, after).start()
-
-            @pl.when(inside & (place == last))
+
+                @pl.when(place < last)
+                def _():
+                    held[stream, at] = (held[stream, at].astype(jnp.float32) + self.own(stream, i)).astype(jnp.bfloat16)
+                    self.acc_copy(stream, i, after).start()
+
+                @pl.when(place == last)
+                def _():
+                    total = held[stream, at].astype(jnp.float32) + self.own(stream, i)
+                    self.out_ref[self.rows_of(stream, i)] = self.finish(stream, i, total).astype(jnp.bfloat16)
+                    self.back_copy(stream, i, before).start()
+
+        back = k - self.hop * (2 * last - place)
+        j = begin + back
+
+        @pl.when((back >= 0) & (back < size) & (place < last))
+        def _():
+            self.back_copy(stream, j, before).wait_recv()
+
+            @pl.when(place > 0)
             def _():
-                self.acc_copy(stream, i, before).wait_recv()
-                total = held[stream, i - self.base].astype(jnp.float32) + self.own(stream, i)
-                self.out_ref[self.rows_of(stream, i)] = self.finish(stream, i, total).astype(jnp.bfloat16)
-                self.back_copy(stream, i, before).start()
-
-            back = k - HOP * (2 * last - place)
-            j = begin + back
-
-            @pl.when((back >= 0) & (back < size) & (place < last))
-            def _():
-                self.back_copy(stream, j, before).wait_recv()
-
-                @pl.when(place > 0)
-                def _():
-                    self.back_copy(stream, j, before).start()
+                self.back_copy(stream, j, before).start()
 
     def drain(self):
         def sent(at, carry):
@@ -155,10 +166,10 @@
         lax.fori_loop(0, self.count, sent, 0)
 
 
-def line_scratch(rows, width, share=1):
-    count = rows // 2 // CHUNK // share
+def line_scratch(rows, width, share=1, chunk=CHUNK):
+    count = rows // 2 // chunk // share
     return [
-        pltpu.VMEM((2, count, CHUNK, width), jnp.bfloat16),
+        pltpu.VMEM((2, count, chunk, width), jnp.bfloat16),
         *[pltpu.SemaphoreType.DMA((2, count))] * 4,
     ]
 
@@ -197,8 +208,8 @@
     pl.semaphore_wait(barrier, peers)
 
 
-def kept_rows(i):
-    return pl.ds(pl.multiple_of(i * CHUNK, CHUNK), CHUNK)
+def kept_rows(i, chunk=CHUNK):
+    return pl.ds(pl.multiple_of(i * chunk, chunk), chunk)
 
 
 def rotate_lanes(values, cosine, signed_sine, back=False):
@@ -573,8 +584,11 @@
 
     def step(k, carry):
         first.step(k)
-        then.step(k - (base_one + work), 0, part)
-        then.step(k - (base_two + work), part, part)
+        if base_two == base_one + part:
+            then.step(k - (base_one + work))
+        else:
+            then.step(k - (base_one + work), 0, part)
+            then.step(k - (base_two + work), part, part)
         third.step(k - third_base)
 
         @pl.when(k == 0)
@@ -813,30 +827,31 @@
         made.wait()
 
     def rows_at(start):
-        return pl.ds(pl.multiple_of(start, CHUNK), CHUNK)
+        return pl.ds(pl.multiple_of(start, BACK_CHUNK), BACK_CHUNK)
 
     def plain(stream, i):
-        return (stream * count + i) * CHUNK
+        return (stream * count + i) * BACK_CHUNK
 
     def finish_out(stream, i, total):
-        return middle[kept_rows(i)] + total
+        return middle[kept_rows(i, BACK_CHUNK)] + total
 
     def finish_in(stream, i, total):
-        hidden = inputs[kept_rows(i)].astype(jnp.float32)
+        hidden = inputs[kept_rows(i, BACK_CHUNK)].astype(jnp.float32)
         inverse = inverse_rms(hidden)
         unit = hidden * inverse
         gain_line[0:1, :] += jnp.sum(total * unit, axis=0, keepdims=True)
         scaled = total * gain_one[...]
-        return grad_middle[kept_rows(i)] + inverse * (
+        return grad_middle[kept_rows(i, BACK_CHUNK)] + inverse * (
             scaled - unit * jnp.mean(scaled * unit, axis=-1, keepdims=True)
         )
 
     out_line = Line(
         n, lambda s, i: layer_out[rows_at(plain(s, i))].astype(jnp.float32), finish_out, plain, layer_out, *line_out,
-        base=count - part,
+        base=count - part, hop=BACK_HOP,
     )
     in_line = Line(
-        n, lambda s, i: grad_inputs[rows_at(plain(s, i))].astype(jnp.float32), finish_in, plain, grad_inputs, *line_in
+        n, lambda s, i: grad_inputs[rows_at(plain(s, i))].astype(jnp.float32), finish_in, plain, grad_inputs, *line_in,
+        hop=BACK_HOP,
     )
 
     def attend_back(side, at, index):
@@ -1000,10 +1015,11 @@
         for r in range(shards - 1):
             spread(r).start()
 
-    lag = tasks + 2
-    ring_steps = [1, 3, 6] + [lag + at for at in range(dp_size - 3)]
+    attend_steps = tasks // TASKS
+    lag = attend_steps + 2
+    ring_steps = RINGS + [lag + at for at in range(dp_size - 3)]
     out_base = lag + 1
-    steps = max(lag + count + 2 * HOP * last, out_base + dp_size)
+    steps = max(lag + count + 2 * BACK_HOP * last, out_base + dp_size)
 
     def step(k, carry):
         out_line.step(k, count - part, part)
@@ -1018,11 +1034,15 @@
             kv_turned[...] = kv[...].T
             grad_mixed[...] = turned_dot(attended[...], out_weight[...]).astype(jnp.bfloat16)
 
-        @pl.when((k >= 1) & (k <= tasks))
-        def _():
-            attend_task(k - 1)
-
-        @pl.when((k == tasks) & (core == 1))
+        @pl.when((k >= 1) & (k <= attend_steps))
+        def _():
+            def task(more, carry):
+                attend_task(TASKS * (k - 1) + more)
+                return carry
+
+            lax.fori_loop(0, TASKS, task, 0)
+
+        @pl.when((k == attend_steps) & (core == 1))
         def _():
             kv_swap().start()
 
@@ -1036,12 +1056,12 @@
             for made in inner_loads:
                 made.wait()
 
-        @pl.when(k == tasks)
+        @pl.when(k == attend_steps)
         def _():
             for made in [*late_loads, *attended_swaps()]:
                 made.wait()
 
-        @pl.when(k == tasks + 1)
+        @pl.when(k == attend_steps + 1)
         def _():
             finish_pre()
             in_products()
@@ -1074,7 +1094,7 @@
             turn(at, normed_cols)
             plane_piece(0, at, pre, grad_qkv)
 
-        @pl.when(k == lag + count + HOP * last - 1)
+        @pl.when(k == lag + count + BACK_HOP * last - 1)
         def _():
             for owner in (0, last):
 
@@ -1083,7 +1103,7 @@
                     for made in line_copies(owner, range(1, n)):
                         made.start()
 
-        @pl.when(k == lag + count + HOP * last + 3)
+        @pl.when(k == min(lag + count + BACK_HOP * last + 3, steps - 1))
         def _():
             gather_gains()
 
@@ -1146,7 +1166,7 @@
         dma((17,)), dma((core_copies,)), dma((core_copies,)),
         dma((dp_size,)), dma((dp_size,)), dma((2, others)), dma((2, others)),
         dma((2, line_size - 1)), dma((2,)), dma((2 * dp_size - 1,)), dma((2 * dp_size - 1,)),
-        *line_scratch(span, width, 2), *line_scratch(span, width),
+        *line_scratch(span, width, 2, BACK_CHUNK), *line_scratch(span, width, 1, BACK_CHUNK),
     ]
     spaces = [outside, outside, vmem, outside, vmem, vmem, vmem] + [outside] * 10 + [vmem, vmem] + [outside] * 4
     return pl.pallas_call(
@@ -1540,7 +1560,7 @@
     dp_size, ctx_size, line_size = mesh.shape["dp"], mesh.shape["ctx"], mesh.shape["tensor"]
     piece = model_width // (dp_size * ctx_size)
     fits = inputs.shape[0] == 1 and ctx_size == 2 and dp_size > 2 and line_size > 1
-    if fits and piece % 128 == 0 and span_len % (2 * CHUNK) == 0:
+    if fits and piece % 128 == 0 and span_len % 512 == 0:
         return fast_body(*arrays)
     return plain_body(*arrays)
 

time: 301 us -> 296 us (0.983)
  Pallas kernels: 300 us -> 295 us
    pallas_call x1, Pallas kernels: 117 us -> 112 us  [back_call(): pl.pallas_call(functools.partial(back_kernel, line_size, dp_size), out_sh...]
where the time goes in v2:
time: 296 us
  Pallas kernels  295 us (100%)
    pallas_call x1, Pallas kernels, front_call(): pl.pallas_call(functools.partial(front_kernel, line_size, dp_size), out_s...  172 us
    pallas_call x1, Pallas kernels, back_call(): pl.pallas_call(functools.partial(back_kernel, line_size, dp_size), out_sh...  112 us
    pallas_call x1, Pallas kernels, settle_call(): pl.pallas_call(settle_kernel, out_shape=[jax.ShapeDtypeStruct(s, d) for s...  10.7 us

profile of v2, /device:TPU:0, one launch (start us, length us, event | category | flops | bytes accessed | tf_op | source)
XLA Modules:
  0.0 296.5 jit_solution(9927570988697998331)
XLA Ops:
  0.7 0.6 reshape_tile.3.frequency
  1.3 171.8 %shard_map.203 = (s32[1,1024]{1,0:T(1,128)}, f32[512,128]{1,0:T(8,128)}, f32[512,128]{1,0:T(8,128)}, bf16[512,512]{1,0:T(8,128)(2,1)}, bf16[1024,128]{1,0:T(8,12...) custom-call(bf16[512,2048]{1,0:T(8,128)(2,1)} %bitcast.12, ...), custom_call_target="tpu_custom_call" | custom-call | tf_op jit(solution)/shard_map/pallas_call | solution.py:742
  173.1 112.5 %shard_map.204 = (bf16[512,2048]{1,0:T(8,128)(2,1)}, bf16[512,2048]{1,0:T(8,128)(2,1)}, f32[8,256]{1,0:T(8,128)}, f32[256,640]{1,0:T(8,128)}, f32[256,512]{1,0:T...) custom-call(bf16[512,512]{1,0:T(8,128)(2,1)} %get-tuple-element.53.q, ...), custom_call_target="tpu_custom_call" | custom-call | tf_op jit(solution)/shard_map/pallas_call | solution.py:1172
  285.6 10.7 %shard_map.205 = (bf16[512,2048]{1,0:T(8,128)(2,1)}, bf16[512,2048]{1,0:T(8,128)(2,1)}, f32[1,256]{1,0:T(1,128)}, f32[256,512]{1,0:T(8,128)}, f32[64,256]{1,0:T(...) custom-call(bf16[512,2048]{1,0:T(8,128)(2,1)} %get-tuple-element.70., ...), custom_call_target="tpu_custom_call" | custom-call | tf_op jit(solution)/shard_map/pallas_call | solution.py:1272
  (2 shorter events, 0.0 us)

commit v3 on v2

--- a/solution.py
+++ b/solution.py
@@ -205,7 +205,7 @@
     elif core:
         call(ctx=1 - side)
         peers += 1
-    pl.semaphore_wait(barrier, peers)
+    return lambda: pl.semaphore_wait(barrier, peers)
 
 
 def kept_rows(i, chunk=CHUNK):
@@ -292,12 +292,11 @@
     ]
     load_up_weight = load(10, up_weight_any, up_weight)
     seg_all[core] = jnp.broadcast_to(segments[...], seg_all.shape[1:])
-    greet(n, True, dp_size)
+    meet = greet(n, True, dp_size)
 
     def seg_copy():
         return remote(seg_all.at[core], seg_all.at[core], core_send.at[1], core_recv.at[1], ctx=1 - core)
 
-    seg_copy().start()
     load_inputs.wait()
 
     def norm_rows(b, carry):
@@ -307,6 +306,16 @@
         return carry
 
     lax.fori_loop(0, span // 64, norm_rows, 0)
+    meet()
+    seg_copy().start()
+    for made in load_kv:
+        made.wait()
+    raw_kv = turned_dot(normed[...], kv_weight[...])
+    load_query.wait()
+    for low in range(0, span, half):
+        rows = slice(low, low + half)
+        partial[rows, 0:heads] = jnp.dot(normed[rows], query_weight[...], preferred_element_type=jnp.float32)
+    load_gate = load(9, gate_weight_any, gate_weight)
     seg_copy().wait()
     for side in (0, 1):
         seg_row[:, side * span : (side + 1) * span] = seg_all[side, 0:1]
@@ -321,11 +330,8 @@
     cosine[...] = jnp.cos(angles)
     sine = jnp.sin(angles)
     signed_sine[...] = jnp.where(lax.rem(lane, HEAD_DIM) < HEAD_DIM // 2, -sine, sine)
-    for made in load_kv:
-        made.wait()
     own_rows = pl.ds(pl.multiple_of(core * span, span), span)
-    raw = turned_dot(normed[...], kv_weight[...])
-    kv[own_rows] = key_lanes(raw, rotate_lanes(raw, cosine[...], signed_sine[...])).astype(jnp.bfloat16)
+    kv[own_rows] = key_lanes(raw_kv, rotate_lanes(raw_kv, cosine[...], signed_sine[...])).astype(jnp.bfloat16)
 
     def kv_copy():
         return remote(kv.at[own_rows], kv.at[own_rows], core_send.at[0], core_recv.at[0], ctx=1 - core)
@@ -338,14 +344,9 @@
     def _():
         kv_copy().start()
 
-    load_query.wait()
-    for low in range(0, span, half):
-        rows = slice(low, low + half)
-        raw = jnp.dot(normed[rows], query_weight[...], preferred_element_type=jnp.float32)
-        for lanes in range(0, raw.shape[1], 128):
-            rotated = rotate_lanes(raw[:, lanes : lanes + 128], cosine[rows], signed_sine[rows])
-            query[rows, lanes : lanes + 128] = rotated.astype(jnp.bfloat16) * (HEAD_DIM ** -0.5)
-    load_gate = load(9, gate_weight_any, gate_weight)
+    for lanes in range(0, heads, 128):
+        rotated = rotate_lanes(partial[:, lanes : lanes + 128], cosine[...], signed_sine[...])
+        query[:, lanes : lanes + 128] = rotated.astype(jnp.bfloat16) * (HEAD_DIM ** -0.5)
 
     @pl.when(core == 1)
     def _():
@@ -530,7 +531,7 @@
     ]
     up_slot = 3 + dp_size + len(far_slots)
     two_moves = [store(7, two_other, two_cols.at[pl.ds(span, span)]), store(5, up, up_out)]
-    second_stores = stores(21, second, second_out)
+    second_stores, attended_stores = stores(21, second, second_out), stores(25, attended, attended_out)
     middle_store = store(29, middle, middle_out)
 
     def gate_swaps():
@@ -678,11 +679,17 @@
             for b in (1, 3):
                 second_stores[b].start()
 
+        @pl.when(k == max(base_one + work, third_base) + part + trip)
+        def _():
+            for b in (0, 2):
+                second_stores[b].start()
+                attended_stores[b].start()
+
         return carry
 
     lax.fori_loop(0, steps, step, 0)
     late_stores = [
-        second_stores[0], second_stores[2], *stores(25, attended, attended_out), store(30, grad_middle, grad_middle_out),
+        attended_stores[1], attended_stores[3], store(30, grad_middle, grad_middle_out),
     ]
     for made in late_stores:
         made.start()
@@ -698,8 +705,8 @@
         for w in ((0, 1) if r < dp_size - 2 else (0,)):
             gate_copy(w, r).wait()
     for made in [
-        *early, mixed_move, *upstream_moves, *hidden_moves, *two_moves, own_store, middle_store, second_stores[1], second_stores[3],
-        *late_stores,
+        *early, mixed_move, *upstream_moves, *hidden_moves, *two_moves, own_store, middle_store, *second_stores,
+        attended_stores[0], attended_stores[2], *late_stores,
     ]:
         made.wait()
 
@@ -781,9 +788,9 @@
         return made
 
     own_half = pl.ds(pl.multiple_of(jnp.where(here == 0, half, 0), half), half)
+    mixed_loads = [load(attended_any, attended), load(out_weight_any, out_weight)]
+    attend_loads = [load(query_any, query), load(kv_any, kv), load(mixed_any, mixed)]
     line_loads = [load(second_any, layer_out), load(middle_any, middle)]
-    mixed_loads = [load(attended_any, attended), load(out_weight_any, out_weight)]
-    attend_loads = [load(query_any, query), load(kv_any, kv)]
 
     up_loads = [load(two_any, two_cols), load(up_any, up)]
     inner_loads = [load(upstream_any, upstream_cols), load(inner_any, inner)]
@@ -791,9 +798,9 @@
         load(query_weight_any, query_weight), load(key_weight_any, kv_weight.at[pl.ds(0, HEAD_DIM)]),
         load(value_weight_any, kv_weight.at[pl.ds(HEAD_DIM, HEAD_DIM)]),
         load(grad_middle_any, grad_middle), load(inputs_any.at[own_half], inputs),
-        load(mixed_any, mixed), load(normed_any, normed_cols),
+        load(normed_any, normed_cols),
     ]
-    greet(n, True, dp_size, full_line=True)
+    meet = greet(n, True, dp_size, full_line=True)
     pre_slot, kv_slot = dp_size, dp_size + 1
 
     def attended_swaps():
@@ -823,8 +830,15 @@
     gain_line[1:2, :] = gain_two_grad[0:1, :]
     kv_grad[...] = jnp.zeros_like(kv_grad)
     seg_col[...] = jnp.broadcast_to(seg_row[...], (8, 2 * span)).T[:, 0:1]
+    for made in [*mixed_loads, *attend_loads]:
+        made.wait()
+    kv_turned[...] = kv[...].T
+    grad_mixed[...] = turned_dot(attended[...], out_weight[...]).astype(jnp.bfloat16)
     for made in line_loads:
         made.wait()
+    meet()
+    for made in attended_swaps():
+        made.start()
 
     def rows_at(start):
         return pl.ds(pl.multiple_of(start, BACK_CHUNK), BACK_CHUNK)
@@ -864,6 +878,7 @@
             fill_bias(bias, seg_col, seg_row, side * span + at * half, keys, half)
 
         both_query, both_grad = query[rows, lanes], grad_mixed[rows, lanes]
+        shared = (both_grad.astype(jnp.float32) * mixed[rows, lanes].astype(jnp.float32)).T
         outs, parts = [], None
         for which in (0, 1):
             head = slice(which * HEAD_DIM, (which + 1) * HEAD_DIM)
@@ -871,8 +886,8 @@
             scores = turned_dot(kv[0:keys, 0:HEAD_DIM], query_head) + bias[0:keys, :]
             probs = jnp.exp(scores - logs[pl.ds(2 * index + which, 1), rows])
             grad_probs = turned_dot(kv[0:keys, HEAD_DIM : 2 * HEAD_DIM], grad_head)
-            both = probs * grad_probs
-            grad_scores = (both - probs * jnp.sum(both, axis=0, keepdims=True)).astype(jnp.bfloat16)
+            row_dot = jnp.sum(shared[head], axis=0, keepdims=True)
+            grad_scores = (probs * (grad_probs - row_dot)).astype(jnp.bfloat16)
             grad_key = jnp.dot(grad_scores, query_head, preferred_element_type=jnp.float32)
             grad_value = jnp.dot(probs.astype(jnp.bfloat16), grad_head, preferred_element_type=jnp.float32)
             part = jnp.concatenate([grad_key, grad_value], axis=1)
@@ -1019,21 +1034,12 @@
     lag = attend_steps + 2
     ring_steps = RINGS + [lag + at for at in range(dp_size - 3)]
     out_base = lag + 1
-    steps = max(lag + count + 2 * BACK_HOP * last, out_base + dp_size)
+    steps = max(lag + count + 2 * BACK_HOP * last, out_base + 2 * dp_size)
 
     def step(k, carry):
         out_line.step(k, count - part, part)
         in_line.step(k - lag)
 
-        @pl.when(k == 0)
-        def _():
-            for made in [*mixed_loads, *attend_loads]:
-                made.wait()
-            for made in attended_swaps():
-                made.start()
-            kv_turned[...] = kv[...].T
-            grad_mixed[...] = turned_dot(attended[...], out_weight[...]).astype(jnp.bfloat16)
-
         @pl.when((k >= 1) & (k <= attend_steps))
         def _():
             def task(more, carry):
@@ -1085,12 +1091,15 @@
         def _():
             pre_swap().wait()
 
-        at = k - out_base
-
-        @pl.when((at >= 0) & (at < dp_size))
+        at, kind = (k - out_base) // 2, lax.rem(k - out_base, 2)
+
+        @pl.when((k >= out_base) & (at < dp_size) & (kind == 0))
         def _():
             turn_attended(at)
             plane_piece(1, at, mixed, own_out)
+
+        @pl.when((k >= out_base) & (at < dp_size) & (kind == 1))
+        def _():
             turn(at, normed_cols)
             plane_piece(0, at, pre, grad_qkv)
 

time: 296 us -> 295 us (level)
  no operation moved by 1% of the time
where the time goes in v3:
time: 295 us
  Pallas kernels  294 us (100%)
    pallas_call x1, Pallas kernels, front_call(): pl.pallas_call(functools.partial(front_kernel, line_size, dp_size), out_s...  173 us
    pallas_call x1, Pallas kernels, back_call(): pl.pallas_call(functools.partial(back_kernel, line_size, dp_size), out_sh...  110 us
    pallas_call x1, Pallas kernels, settle_call(): pl.pallas_call(settle_kernel, out_shape=[jax.ShapeDtypeStruct(s, d) for s...  10.7 us

profile of v3, /device:TPU:0, one launch (start us, length us, event | category | flops | bytes accessed | tf_op | source)
XLA Modules:
  0.0 295.2 jit_solution(11384083218113987033)
XLA Ops:
  0.7 0.6 reshape_tile.3.frequency
  1.3 172.7 %shard_map.203 = (s32[1,1024]{1,0:T(1,128)}, f32[512,128]{1,0:T(8,128)}, f32[512,128]{1,0:T(8,128)}, bf16[512,512]{1,0:T(8,128)(2,1)}, bf16[1024,128]{1,0:T(8,12...) custom-call(bf16[512,2048]{1,0:T(8,128)(2,1)} %bitcast.12, ...), custom_call_target="tpu_custom_call" | custom-call | tf_op jit(solution)/shard_map/pallas_call | solution.py:749
  174.0 110.3 %shard_map.204 = (bf16[512,2048]{1,0:T(8,128)(2,1)}, bf16[512,2048]{1,0:T(8,128)(2,1)}, f32[8,256]{1,0:T(8,128)}, f32[256,640]{1,0:T(8,128)}, f32[256,512]{1,0:T...) custom-call(bf16[512,512]{1,0:T(8,128)(2,1)} %get-tuple-element.53.q, ...), custom_call_target="tpu_custom_call" | custom-call | tf_op jit(solution)/shard_map/pallas_call | solution.py:1181
  284.3 10.7 %shard_map.205 = (bf16[512,2048]{1,0:T(8,128)(2,1)}, bf16[512,2048]{1,0:T(8,128)(2,1)}, f32[1,256]{1,0:T(1,128)}, f32[256,512]{1,0:T(8,128)}, f32[64,256]{1,0:T(...) custom-call(bf16[512,2048]{1,0:T(8,128)(2,1)} %get-tuple-element.70., ...), custom_call_target="tpu_custom_call" | custom-call | tf_op jit(solution)/shard_map/pallas_call | solution.py:1281
  (2 shorter events, 0.0 us)

commit v4 on v3

--- a/solution.py
+++ b/solution.py
@@ -650,14 +650,14 @@
             for made in gate_swaps():
                 made.start()
 
-        @pl.when(k == base_two + work + 1)
+        @pl.when(k == base_two + work)
         def _():
             for made in gate_swaps():
                 made.wait()
             for made in two_moves:
                 made.start()
 
-        gate_task = k - (base_two + work + 1)
+        gate_task = k - (base_two + work)
 
         @pl.when((gate_task >= 0) & (gate_task < dp_size - 1))
         def _():
@@ -1215,11 +1215,11 @@
         )
         for at, (own, far) in enumerate(zip(owns, fars))
     ]
-    for pair in loads:
-        for made in pair:
-            made.start()
     for made in passed:
         made.start()
+    for at in (4, 2, 3, 0, 1):
+        for made in loads[at]:
+            made.start()
     gain_one[...] = gains[0:1]
     gain_two[...] = gains[1:2]
 
@@ -1237,6 +1237,17 @@
         whole.append(made)
 
     heads = grad_query.shape[1]
+    passed[0].wait()
+    put(0, layer_held, layer_out)
+    passed[1].wait()
+    put(1, inputs_held, grad_inputs)
+    turned_down[...] = settle(4, own_down, far_down).T
+    put(8, turned_down, grad_down)
+    own_gate[...] = settle(2, own_gate, far_gate)
+    put(6, own_gate, grad_gate)
+    passed[2].wait()
+    own_up[...] = settle(3, own_up, far_up)
+    put(7, own_up, grad_up)
     own_qkv[...] = settle(0, own_qkv, far_qkv)
     put(2, own_qkv.at[:, pl.ds(0, heads)], grad_query)
     turned_kv[...] = own_qkv[:, heads:].T
@@ -1244,17 +1255,6 @@
     put(4, turned_kv.at[pl.ds(HEAD_DIM, HEAD_DIM)], grad_value)
     turned_out[...] = settle(1, own_out, far_out).T
     put(5, turned_out, grad_out)
-    passed[0].wait()
-    put(0, layer_held, layer_out)
-    own_gate[...] = settle(2, own_gate, far_gate)
-    put(6, own_gate, grad_gate)
-    passed[2].wait()
-    own_up[...] = settle(3, own_up, far_up)
-    put(7, own_up, grad_up)
-    passed[1].wait()
-    put(1, inputs_held, grad_inputs)
-    turned_down[...] = settle(4, own_down, far_down).T
-    put(8, turned_down, grad_down)
     for made in whole:
         made.wait()
 

time: 295 us -> 295 us (level)
  no operation moved by 1% of the time
where the time goes in v4:
time: 295 us
  Pallas kernels  294 us (100%)
    pallas_call x1, Pallas kernels, front_call(): pl.pallas_call(functools.partial(front_kernel, line_size, dp_size), out_s...  172 us
    pallas_call x1, Pallas kernels, back_call(): pl.pallas_call(functools.partial(back_kernel, line_size, dp_size), out_sh...  110 us
    pallas_call x1, Pallas kernels, settle_call(): pl.pallas_call(settle_kernel, out_shape=[jax.ShapeDtypeStruct(s, d) for s...  11.2 us

profile of v4, /device:TPU:0, one launch (start us, length us, event | category | flops | bytes accessed | tf_op | source)
XLA Modules:
  0.0 295.2 jit_solution(3409587846991923977)
XLA Ops:
  0.7 0.6 reshape_tile.3.frequency
  1.3 172.2 %shard_map.203 = (s32[1,1024]{1,0:T(1,128)}, f32[512,128]{1,0:T(8,128)}, f32[512,128]{1,0:T(8,128)}, bf16[512,512]{1,0:T(8,128)(2,1)}, bf16[1024,128]{1,0:T(8,12...) custom-call(bf16[512,2048]{1,0:T(8,128)(2,1)} %bitcast.12, ...), custom_call_target="tpu_custom_call" | custom-call | tf_op jit(solution)/shard_map/pallas_call | solution.py:749
  173.5 110.3 %shard_map.204 = (bf16[512,2048]{1,0:T(8,128)(2,1)}, bf16[512,2048]{1,0:T(8,128)(2,1)}, f32[8,256]{1,0:T(8,128)}, f32[256,640]{1,0:T(8,128)}, f32[256,512]{1,0:T...) custom-call(bf16[512,512]{1,0:T(8,128)(2,1)} %get-tuple-element.53.q, ...), custom_call_target="tpu_custom_call" | custom-call | tf_op jit(solution)/shard_map/pallas_call | solution.py:1181
  283.8 11.2 %shard_map.205 = (bf16[512,2048]{1,0:T(8,128)(2,1)}, bf16[512,2048]{1,0:T(8,128)(2,1)}, f32[1,256]{1,0:T(1,128)}, f32[256,512]{1,0:T(8,128)}, f32[64,256]{1,0:T(...) custom-call(bf16[512,2048]{1,0:T(8,128)(2,1)} %get-tuple-element.70., ...), custom_call_target="tpu_custom_call" | custom-call | tf_op jit(solution)/shard_map/pallas_call | solution.py:1281
  (2 shorter events, 0.0 us)

commit v5 on v3

--- a/solution.py
+++ b/solution.py
@@ -650,14 +650,14 @@
             for made in gate_swaps():
                 made.start()
 
-        @pl.when(k == base_two + work + 1)
+        @pl.when(k == base_two + work)
         def _():
             for made in gate_swaps():
                 made.wait()
             for made in two_moves:
                 made.start()
 
-        gate_task = k - (base_two + work + 1)
+        gate_task = k - (base_two + work)
 
         @pl.when((gate_task >= 0) & (gate_task < dp_size - 1))
         def _():

time: 295 us -> 295 us (level)
  no operation moved by 1% of the time
where the time goes in v5:
time: 295 us
  Pallas kernels  293 us (99%)
    pallas_call x1, Pallas kernels, front_call(): pl.pallas_call(functools.partial(front_kernel, line_size, dp_size), out_s...  172 us
    pallas_call x1, Pallas kernels, back_call(): pl.pallas_call(functools.partial(back_kernel, line_size, dp_size), out_sh...  110 us
    pallas_call x1, Pallas kernels, settle_call(): pl.pallas_call(settle_kernel, out_shape=[jax.ShapeDtypeStruct(s, d) for s...  10.7 us

profile of v5, /device:TPU:0, one launch (start us, length us, event | category | flops | bytes accessed | tf_op | source)
XLA Modules:
  0.0 294.7 jit_solution(6870591621733558455)
XLA Ops:
  0.7 0.6 reshape_tile.3.frequency
  1.3 172.2 %shard_map.203 = (s32[1,1024]{1,0:T(1,128)}, f32[512,128]{1,0:T(8,128)}, f32[512,128]{1,0:T(8,128)}, bf16[512,512]{1,0:T(8,128)(2,1)}, bf16[1024,128]{1,0:T(8,12...) custom-call(bf16[512,2048]{1,0:T(8,128)(2,1)} %bitcast.12, ...), custom_call_target="tpu_custom_call" | custom-call | tf_op jit(solution)/shard_map/pallas_call | solution.py:749
  173.5 110.3 %shard_map.204 = (bf16[512,2048]{1,0:T(8,128)(2,1)}, bf16[512,2048]{1,0:T(8,128)(2,1)}, f32[8,256]{1,0:T(8,128)}, f32[256,640]{1,0:T(8,128)}, f32[256,512]{1,0:T...) custom-call(bf16[512,512]{1,0:T(8,128)(2,1)} %get-tuple-element.53.q, ...), custom_call_target="tpu_custom_call" | custom-call | tf_op jit(solution)/shard_map/pallas_call | solution.py:1181
  283.8 10.7 %shard_map.205 = (bf16[512,2048]{1,0:T(8,128)(2,1)}, bf16[512,2048]{1,0:T(8,128)(2,1)}, f32[1,256]{1,0:T(1,128)}, f32[256,512]{1,0:T(8,128)}, f32[64,256]{1,0:T(...) custom-call(bf16[512,2048]{1,0:T(8,128)(2,1)} %get-tuple-element.70., ...), custom_call_target="tpu_custom_call" | custom-call | tf_op jit(solution)/shard_map/pallas_call | solution.py:1281
  (2 shorter events, 0.0 us)
